TPU v7x, 128 devices: a whole 4x4x4 slice. The times are simulated.
128 devices in a mesh: dp: 16 (over x, z_hi, core), proto: 8 (over y, z_lo).
Axes of the slice: x: 4, y: 4, z: 4 (z_hi: 2, z_lo: 2; z = z_hi * 2 + z_lo), core: 2. Of those that a mesh axis runs over, the one named last changes fastest.
Arguments:
- student_feats: float32 [2560, 256], P('dp'), may hold values from -6 to 6
- teacher_feats: float32 [512, 256], P('dp'), may hold values from -6 to 6
- student_proto: float32 [256, 65536], P('dp', 'proto'), may hold values from -6 to 6
- teacher_proto: float32 [256, 65536], P('dp', 'proto'), may hold values from -6 to 6
- crops: int32 [2560, 2], P('dp'), may hold values from 0 to 15, as said below
- step: int32 [1], replicated, may hold values from 0 to 24999
Outputs:
- student_next: float32 [256, 65536], P('dp', 'proto')
- teacher_next: float32 [256, 65536], P('dp', 'proto')
- feature_grad: float32 [2560, 256], P('dp')
Inputs may be any that keep to these rules, and one draw needn't show every extreme that they name: Within each device's block of 160 rows every pair (image i < 16, slot c < 10) appears exactly once; slots below 2 are the global crops, slot g of image i being the same crop as teacher row 2 * i + g of that block.
All inputs are finite; a program needn't handle non-finite values.
Results may differ from a plain program's by a relative error of at most 0.0003.
Values sent between devices are 32-bit elements; how exact they have to be, the bound alone decides.
No kernel may reach another device: no remote copies, remote signals or barrier semaphores. Data moves between devices by JAX's collectives and lax.ppermute only.
A program may use at most 128 MiB of HBM per device.

v0:
```python
import jax
import jax.numpy as jnp
from jax import lax
from jax.sharding import PartitionSpec as P

CROPS = 10
GLOBAL_CROPS = 2
ITERS = 3
WARM_STEPS = 12500
TOTAL_STEPS = 625000


student_temp = 0.1
loss_scale = 16777216.0
norm_eps = 1e-06
square_eps = 1e-06
rate_peak = 0.05
weight_decay = 0.04
momentum_base = 0.994
highest = lax.Precision.HIGHEST


def side_by_side(arrays, axis, dim, along):
    both = jnp.concatenate(arrays, axis=along)
    result, at, outs = (lax.all_gather(both, axis, axis=dim, tiled=True), 0, [])
    for a in arrays:
        outs.append(lax.slice_in_dim(result, at, at + a.shape[along], axis=along))
        at += a.shape[along]
    return tuple(outs)


def from_everyone(x, axis):
    copies = jnp.broadcast_to(x, (lax.axis_size(axis), *x.shape))
    return lax.all_to_all(copies, axis, split_axis=0, concat_axis=0, tiled=True)


def taken_together(x, axis):
    everything = from_everyone(x, axis)
    return jnp.sum(everything, axis=0)


def together(arrays, axis):
    flat, at, outs = (jnp.concatenate([a.reshape(-1) for a in arrays]), 0, [])
    so_far = taken_together(flat, axis)
    for a in arrays:
        outs.append(so_far[at : at + a.size].reshape(a.shape))
        at += a.size
    return tuple(outs)


def plan(step):
    value = step[0].astype(jnp.float32)
    ramp = jnp.minimum(1.0, value / WARM_STEPS)
    rate = rate_peak * (0.25 + 0.75 * ramp)
    teacher_temp = 0.04 + 0.03 * ramp
    momentum = 1.0 - (1.0 - momentum_base) * (jnp.cos(jnp.pi * value / TOTAL_STEPS) + 1.0) * 0.5
    return (rate, teacher_temp, momentum)


def unit_rows(values):
    norm = jnp.sqrt(jnp.sum(values * values, axis=1, keepdims=True) + norm_eps)
    return (values / norm, norm)


def unit_columns(values):
    norm = jnp.sqrt(jnp.sum(values * values, axis=0, keepdims=True) + norm_eps)
    return (values / norm, norm)


def body(student_feats, teacher_feats, student_proto, teacher_proto, crops, step):
    rate, teacher_temp, momentum = plan(step)
    full_student, full_teacher = side_by_side((student_proto, teacher_proto), "dp", 0, 1)
    student_unit, student_norm = unit_columns(full_student)
    teacher_unit, teacher_norm = unit_columns(full_teacher)
    t_unit, t_norm = unit_rows(teacher_feats)
    s_unit, s_norm = unit_rows(student_feats)
    crop_rows, width = s_unit.shape
    teach_rows = t_unit.shape[0]
    blocks = crop_rows // teach_rows
    row_blocks = s_unit.reshape(blocks, teach_rows, width)

    def block_expo(rows):
        logits = (
            jnp.dot(rows, student_unit, precision=highest, preferred_element_type=jnp.float32)
            / student_temp
        )
        return jnp.exp(logits)

    expo_blocks = lax.map(block_expo, row_blocks)
    student_total = jnp.sum(expo_blocks, axis=2).reshape(crop_rows)
    assign = jnp.exp(
        jnp.dot(t_unit, teacher_unit, precision=highest, preferred_element_type=jnp.float32)
        / teacher_temp
    )
    for turn in range(ITERS):
        column = taken_together(jnp.sum(assign, axis=0), "dp")
        assign = assign / column[None, :]
        row_part = jnp.sum(assign, axis=1)
        if turn == 0:
            row, student_total = together((row_part, student_total), "proto")
        else:
            row = taken_together(row_part, "proto")
        assign = assign / row[:, None]
    images = teach_rows // GLOBAL_CROPS * lax.axis_size("dp")
    pair_total = GLOBAL_CROPS * (GLOBAL_CROPS - 1) + (CROPS - GLOBAL_CROPS) * GLOBAL_CROPS
    coef = loss_scale / (pair_total * images * student_temp)
    teach_iota = lax.broadcasted_iota(jnp.int32, (1, teach_rows), 1)
    same = crops[:, 0:1] == teach_iota // GLOBAL_CROPS
    other = crops[:, 1:2] != teach_iota % GLOBAL_CROPS
    pairs = jnp.where(same & other, 1.0, 0.0).astype(jnp.float32)
    pair_blocks = pairs.reshape(blocks, teach_rows, teach_rows)
    total_blocks = student_total.reshape(blocks, teach_rows, 1)

    def grad_block(carry, pieces):
        rows, expo, pair_rows, total = pieces
        prob = expo / total
        target = jnp.dot(pair_rows, assign, precision=highest, preferred_element_type=jnp.float32)
        count = jnp.sum(pair_rows, axis=1, keepdims=True)
        dscore = coef * (count * prob - target)
        carry = carry + jnp.dot(
            rows.T, dscore, precision=highest, preferred_element_type=jnp.float32
        )
        back = jnp.dot(
            dscore, student_unit.T, precision=highest, preferred_element_type=jnp.float32
        )
        return (carry, back)

    start_grad = jnp.zeros(student_unit.shape, jnp.float32)
    grad_unit, backs = lax.scan(
        grad_block, start_grad, (row_blocks, expo_blocks, pair_blocks, total_blocks)
    )
    feature_part = backs.reshape(crop_rows, width)
    feature_unit = taken_together(feature_part, "proto")
    feature_grad = (
        feature_unit - s_unit * jnp.sum(s_unit * feature_unit, axis=1, keepdims=True)
    ) / s_norm
    own_rows = student_proto.shape[0]
    first = lax.axis_index("dp") * own_rows
    own_unit = lax.dynamic_slice_in_dim(student_unit, first, own_rows, 0)
    part_grad = lax.psum_scatter(grad_unit, "dp", scatter_dimension=0, tiled=True)
    along_part = jnp.sum(own_unit * part_grad, axis=0)
    squares_part = jnp.sum(part_grad * part_grad, axis=0)
    along, squares = together((along_part, squares_part), "dp")
    proto_grad = (part_grad - own_unit * along[None, :]) / student_norm
    square = (squares - along * along)[None, :] / (student_norm * student_norm * width)
    direction = proto_grad / jnp.sqrt(square + square_eps)
    student_next = student_proto - rate * (direction + weight_decay * student_proto)
    teacher_next = momentum * teacher_proto + (1.0 - momentum) * student_next
    return (student_next, teacher_next, feature_grad)


def solution(mesh):
    in_specs = (
        P("dp", None),
        P("dp", None),
        P("dp", "proto"),
        P("dp", "proto"),
        P("dp", None),
        P(),
    )
    out_specs = (P("dp", "proto"), P("dp", "proto"), P("dp", None))
    return jax.shard_map(body, mesh=mesh, in_specs=in_specs, out_specs=out_specs, check_vma=False)
```

profile of v0, /device:TPU:1, one launch (start us, length us, event | category | flops | bytes accessed | tf_op | source)
XLA Modules:
  0.0 507.3 jit_solution(2299026307607051905)
XLA Ops:
  13.1 110.7 %all-gather.2.cloned.1.call-done = f32[256,16384]{1,0:T(8,128)} async-done(((f32[16,16384]{1,0:T(8,128)}), f32[256,16384]{1,0:T(8,128)}) %all-gather.2.cloned.1.call-update) | async-done | bytes 16777232 | tf_op jit(solution)/shard_map/all_gather | solution.py:25
  123.8 6.6 %multiply_reduce_fusion = (f32[8192]{0:T(1024)S(1)}, f32[8192]{0:T(1024)S(1)}) fusion(f32[256,16384]{1,0:T(8,128)} %all-gather.2.cloned.1.call-done), kind=kLoop, calls=%fused_computation.25 | loop fusion | flops 8372224 | bytes 16842752 | tf_op jit(solution)/shard_map/reduce_sum | solution.py:66
  130.4 4.0 copy-done.1
  134.4 5.2 %fusion.38 = (f32[8192]{0:T(1024)S(1)}, f32[32,8192]{1,0:T(8,128)S(1)}) fusion(f32[]{:T(128)} %bitcast.4, f32[256,16384]{1,0:T(8,128)S(1)} %copy-done.1, f32[8192]{0:T(1024)S(1)} %add_sqrt_fusion, f32[32,256]{1,0:T(8,128)S(1)} %copy-done.4, f32[32]{0:T(128)S(1)} %add_sqrt_fusion.3), kind=kOutput, calls=%fused_computation.77 | convolution fusion | flops 807927808 | bytes 9536004 | tf_op jit(solution)/shard_map/dot_general | solution.py:92
  144.5 7.8 %slice_divide_fusion = f32[256,8192]{1,0:T(8,128)} fusion(f32[256,16384]{1,0:T(8,128)} %all-gather.2.cloned.1.call-done, f32[8192]{0:T(1024)S(1)} %add_sqrt_fusion.1), kind=kLoop, calls=%fused_computation.29 | loop fusion | flops 2097152 | bytes 16809984 | tf_op jit(solution)/shard_map/div | solution.py:67
  152.2 46.2 %while.23 = (s32[]{:T(128)}, f32[5,32,8192]{2,1,0:T(8,128)}, f32[5,32,256]{2,1,0:T(8,128)S(1)}, f32[256,8192]{1,0:T(8,128)}, s32[]{:T(128)}) while((s32[]{:T(128)}, f32[5,32,8192]{2,1,0:T(8,128)}, f32[5,32,256]{2,1,0:T(8,128)S(1)}, f32[256,8192]{1,0:T(8,128)}, s32[]{:T(128)}) %tuple.57), condition=%wide.region_3.0_spmd, body=%wide.region_2.0_spmd.sunk | while | flops 805568512 | bytes 9471037 | solution.py:89
  152.2 9.3 %fusion.58 = f32[5,32,8192]{2,1,0:T(8,128)} fusion(f32[5,32,8192]{2,1,0:T(8,128)} %get-tuple-element.232, s32[]{:T(128)} %get-tuple-element.231, f32[256,8192]{1,0:T(8,128)} %get-tuple-element.239, f32[5,32,256]{2,1,0:T(8,128)S(1)} %get-tuple-element.238), kind=kOutput, calls=%fused_computation.3.clone.1 | convolution fusion | flops 805568512 | bytes 9470976 | tf_op jit(solution)/shard_map/while/body/eval_jaxpr/dot_general | solution.py:84
  161.5 9.2 %fusion.58 = f32[5,32,8192]{2,1,0:T(8,128)} fusion(f32[5,32,8192]{2,1,0:T(8,128)} %get-tuple-element.232, s32[]{:T(128)} %get-tuple-element.231, f32[256,8192]{1,0:T(8,128)} %get-tuple-element.239, f32[5,32,256]{2,1,0:T(8,128)S(1)} %get-tuple-element.238), kind=kOutput, calls=%fused_computation.3.clone.1 | convolution fusion | flops 805568512 | bytes 9470976 | tf_op jit(solution)/shard_map/while/body/eval_jaxpr/dot_general | solution.py:84
  170.7 9.2 %fusion.58 = f32[5,32,8192]{2,1,0:T(8,128)} fusion(f32[5,32,8192]{2,1,0:T(8,128)} %get-tuple-element.232, s32[]{:T(128)} %get-tuple-element.231, f32[256,8192]{1,0:T(8,128)} %get-tuple-element.239, f32[5,32,256]{2,1,0:T(8,128)S(1)} %get-tuple-element.238), kind=kOutput, calls=%fused_computation.3.clone.1 | convolution fusion | flops 805568512 | bytes 9470976 | tf_op jit(solution)/shard_map/while/body/eval_jaxpr/dot_general | solution.py:84
  179.9 9.2 %fusion.58 = f32[5,32,8192]{2,1,0:T(8,128)} fusion(f32[5,32,8192]{2,1,0:T(8,128)} %get-tuple-element.232, s32[]{:T(128)} %get-tuple-element.231, f32[256,8192]{1,0:T(8,128)} %get-tuple-element.239, f32[5,32,256]{2,1,0:T(8,128)S(1)} %get-tuple-element.238), kind=kOutput, calls=%fused_computation.3.clone.1 | convolution fusion | flops 805568512 | bytes 9470976 | tf_op jit(solution)/shard_map/while/body/eval_jaxpr/dot_general | solution.py:84
  189.1 9.3 %fusion.58 = f32[5,32,8192]{2,1,0:T(8,128)} fusion(f32[5,32,8192]{2,1,0:T(8,128)} %get-tuple-element.232, s32[]{:T(128)} %get-tuple-element.231, f32[256,8192]{1,0:T(8,128)} %get-tuple-element.239, f32[5,32,256]{2,1,0:T(8,128)S(1)} %get-tuple-element.238), kind=kOutput, calls=%fused_computation.3.clone.1 | convolution fusion | flops 805568512 | bytes 9470976 | tf_op jit(solution)/shard_map/while/body/eval_jaxpr/dot_general | solution.py:84
  202.0 8.9 %all_to_all.47 = f32[8,1,192]{2,1,0:T(1,128)S(1)} all-to-all(f32[8,1,192]{2,1,0:T(1,128)S(1)} %broadcast_in_dim.69), channel_id=1, replica_groups=mesh['dp'=16,'proto'=8] {'proto'}, dimensions={0} | all-to-all | bytes 12288 | tf_op jit(solution)/shard_map/all_to_all | solution.py:34
  211.7 20.3 %all_to_all.48 = f32[16,1,8192]{2,1,0:T(1,128)S(1)} all-to-all(f32[16,1,8192]{2,1,0:T(1,128)S(1)} %broadcast_in_dim.70), channel_id=1, replica_groups=mesh['dp'=16,'proto'=8] {'dp'}, dimensions={0} | all-to-all | bytes 1048576 | tf_op jit(solution)/shard_map/all_to_all | solution.py:34
  232.7 7.4 %all_to_all.49 = f32[8,1,32]{2,1,0:T(1,128)S(1)} all-to-all(f32[8,1,32]{2,1,0:T(1,128)S(1)} %broadcast_in_dim.71), channel_id=1, replica_groups=mesh['dp'=16,'proto'=8] {'proto'}, dimensions={0} | all-to-all | bytes 2048 | tf_op jit(solution)/shard_map/all_to_all | solution.py:34
  241.7 5.7 %all-to-all-start.4 = ((f32[16,1,8192]{2,1,0:T(1,128)}), f32[16,1,8192]{2,1,0:T(1,128)S(1)}, u32[]{:S(2)}, u32[]{:S(2)}) async-start(f32[16,1,8192]{2,1,0:T(1,128)} %broadcast_in_dim.72), calls=%async_computation.4 | async-start | bytes 1048576 | tf_op jit(solution)/shard_map/all_to_all | solution.py:34
  247.6 11.1 %all-to-all-done.4 = f32[16,1,8192]{2,1,0:T(1,128)S(1)} async-done(((f32[16,1,8192]{2,1,0:T(1,128)}), f32[16,1,8192]{2,1,0:T(1,128)S(1)}, u32[]{:S(2)}, u32[]{:S(2)}) %all-to-all-start.4) | async-done | bytes 524320 | tf_op jit(solution)/shard_map/all_to_all | solution.py:34
  263.7 4.5 all-to-all-done.5
  268.6 104.6 %while.24 = (s32[]{:T(128)}, f32[256,8192]{1,0:T(8,128)}, f32[5,32,256]{2,1,0:T(8,128)S(1)}, f32[5,32,256]{2,1,0:T(8,128)S(1)}, f32[5,32,32]{2,1,0:T(8,128)S(1)}...) while((s32[]{:T(128)}, f32[256,8192]{1,0:T(8,128)}, ...), condition=%wide.region_21.22_spmd.clone, body=%wide.region_19.21_spmd.clone.sunk | while | flops 1716519936 | bytes 64051744 | solution.py:129
  271.1 9.2 %convolution_add_fusion.2 = f32[256,8192]{1,0:T(8,128)} fusion(f32[32,8192]{1,0:T(8,128)S(1)} %fusion.66, f32[256,8192]{1,0:T(8,128)} %get-tuple-element.253, pred[]{:T(512)S(6)} %compare.10, f32[5,32,256]{2,1,0:T(8,128)S(1)} %get-tuple-element.266, s32[]{:T(128)} %get-tuple-element.252), kind=kOutput, calls=%fused_computation.7.clone.1 | convolution fusion | flops 809500672 | bytes 17858564 | tf_op jit(solution)/shard_map/while/body/eval_jaxpr/dot_general | solution.py:120
  280.3 7.4 %fusion.67 = f32[5,32,256]{2,1,0:T(8,128)S(1)} fusion(f32[5,32,256]{2,1,0:T(8,128)S(1)} %get-tuple-element.254, s32[]{:T(128)} %get-tuple-element.252, f32[32,8192]{1,0:T(8,128)S(1)} %fusion.66, f32[256,8192]{1,0:T(8,128)S(1)} %copy-done), kind=kOutput, calls=%fused_computation.11.clone.1 | convolution fusion | flops 805306368 | bytes 9469956 | tf_op jit(solution)/shard_map/while/body/eval_jaxpr/dot_general | solution.py:123
  290.2 11.5 %convolution_add_fusion.2 = f32[256,8192]{1,0:T(8,128)} fusion(f32[32,8192]{1,0:T(8,128)S(1)} %fusion.66, f32[256,8192]{1,0:T(8,128)} %get-tuple-element.253, pred[]{:T(512)S(6)} %compare.10, f32[5,32,256]{2,1,0:T(8,128)S(1)} %get-tuple-element.266, s32[]{:T(128)} %get-tuple-element.252), kind=kOutput, calls=%fused_computation.7.clone.1 | convolution fusion | flops 809500672 | bytes 17858564 | tf_op jit(solution)/shard_map/while/body/eval_jaxpr/dot_general | solution.py:120
  301.7 7.4 %fusion.67 = f32[5,32,256]{2,1,0:T(8,128)S(1)} fusion(f32[5,32,256]{2,1,0:T(8,128)S(1)} %get-tuple-element.254, s32[]{:T(128)} %get-tuple-element.252, f32[32,8192]{1,0:T(8,128)S(1)} %fusion.66, f32[256,8192]{1,0:T(8,128)S(1)} %copy-done), kind=kOutput, calls=%fused_computation.11.clone.1 | convolution fusion | flops 805306368 | bytes 9469956 | tf_op jit(solution)/shard_map/while/body/eval_jaxpr/dot_general | solution.py:123
  311.5 11.5 %convolution_add_fusion.2 = f32[256,8192]{1,0:T(8,128)} fusion(f32[32,8192]{1,0:T(8,128)S(1)} %fusion.66, f32[256,8192]{1,0:T(8,128)} %get-tuple-element.253, pred[]{:T(512)S(6)} %compare.10, f32[5,32,256]{2,1,0:T(8,128)S(1)} %get-tuple-element.266, s32[]{:T(128)} %get-tuple-element.252), kind=kOutput, calls=%fused_computation.7.clone.1 | convolution fusion | flops 809500672 | bytes 17858564 | tf_op jit(solution)/shard_map/while/body/eval_jaxpr/dot_general | solution.py:120
  323.1 7.4 %fusion.67 = f32[5,32,256]{2,1,0:T(8,128)S(1)} fusion(f32[5,32,256]{2,1,0:T(8,128)S(1)} %get-tuple-element.254, s32[]{:T(128)} %get-tuple-element.252, f32[32,8192]{1,0:T(8,128)S(1)} %fusion.66, f32[256,8192]{1,0:T(8,128)S(1)} %copy-done), kind=kOutput, calls=%fused_computation.11.clone.1 | convolution fusion | flops 805306368 | bytes 9469956 | tf_op jit(solution)/shard_map/while/body/eval_jaxpr/dot_general | solution.py:123
  332.9 11.5 %convolution_add_fusion.2 = f32[256,8192]{1,0:T(8,128)} fusion(f32[32,8192]{1,0:T(8,128)S(1)} %fusion.66, f32[256,8192]{1,0:T(8,128)} %get-tuple-element.253, pred[]{:T(512)S(6)} %compare.10, f32[5,32,256]{2,1,0:T(8,128)S(1)} %get-tuple-element.266, s32[]{:T(128)} %get-tuple-element.252), kind=kOutput, calls=%fused_computation.7.clone.1 | convolution fusion | flops 809500672 | bytes 17858564 | tf_op jit(solution)/shard_map/while/body/eval_jaxpr/dot_general | solution.py:120
  344.4 7.4 %fusion.67 = f32[5,32,256]{2,1,0:T(8,128)S(1)} fusion(f32[5,32,256]{2,1,0:T(8,128)S(1)} %get-tuple-element.254, s32[]{:T(128)} %get-tuple-element.252, f32[32,8192]{1,0:T(8,128)S(1)} %fusion.66, f32[256,8192]{1,0:T(8,128)S(1)} %copy-done), kind=kOutput, calls=%fused_computation.11.clone.1 | convolution fusion | flops 805306368 | bytes 9469956 | tf_op jit(solution)/shard_map/while/body/eval_jaxpr/dot_general | solution.py:123
  354.3 11.5 %convolution_add_fusion.2 = f32[256,8192]{1,0:T(8,128)} fusion(f32[32,8192]{1,0:T(8,128)S(1)} %fusion.66, f32[256,8192]{1,0:T(8,128)} %get-tuple-element.253, pred[]{:T(512)S(6)} %compare.10, f32[5,32,256]{2,1,0:T(8,128)S(1)} %get-tuple-element.266, s32[]{:T(128)} %get-tuple-element.252), kind=kOutput, calls=%fused_computation.7.clone.1 | convolution fusion | flops 809500672 | bytes 17858564 | tf_op jit(solution)/shard_map/while/body/eval_jaxpr/dot_general | solution.py:120
  365.8 7.4 %fusion.67 = f32[5,32,256]{2,1,0:T(8,128)S(1)} fusion(f32[5,32,256]{2,1,0:T(8,128)S(1)} %get-tuple-element.254, s32[]{:T(128)} %get-tuple-element.252, f32[32,8192]{1,0:T(8,128)S(1)} %fusion.66, f32[256,8192]{1,0:T(8,128)S(1)} %copy-done), kind=kOutput, calls=%fused_computation.11.clone.1 | convolution fusion | flops 805306368 | bytes 9469956 | tf_op jit(solution)/shard_map/while/body/eval_jaxpr/dot_general | solution.py:123
  374.5 3.8 all-to-all-start.7
  378.3 92.7 %reduce-scatter.2.cloned.1.call-done = f32[16,8192]{1,0:T(8,128)} async-done(((f32[256,8192]{1,0:T(8,128)}), f32[16,8192]{1,0:T(8,128)}) %reduce-scatter.2.cloned.1.call-update) | async-done | bytes 524304 | tf_op jit(solution)/shard_map/reduce_scatter | solution.py:140
  474.4 5.9 %all-to-all-start.6 = ((f32[16,1,16384]{2,1,0:T(1,128)}), f32[16,1,16384]{2,1,0:T(1,128)S(1)}, u32[]{:S(2)}, u32[]{:S(2)}) async-start(f32[16,1,16384]{2,1,0:T(1,128)} %broadcast_in_dim.74), calls=%async_computation.7 | async-start | bytes 2097152 | tf_op jit(solution)/shard_map/all_to_all | solution.py:34
  481.4 15.8 %all-to-all-done.6 = f32[16,1,16384]{2,1,0:T(1,128)S(1)} async-done(((f32[16,1,16384]{2,1,0:T(1,128)}), f32[16,1,16384]{2,1,0:T(1,128)S(1)}, u32[]{:S(2)}, u32[]{:S(2)}) %all-to-all-start.6) | async-done | bytes 1048608 | tf_op jit(solution)/shard_map/all_to_all | solution.py:34
  (92 shorter events, 43.3 us)
Async XLA Ops:
  7.2 116.6 %all-gather.2.cloned.1.call-start = ((), (), s32[]{:S(2)}) async-start(), calls=%async_computation.9 | async-start | bytes 17825792 | tf_op jit(solution)/shard_map/all_gather | solution.py:25
  13.1 117.3 %copy-start.4 = (f32[32,256]{1,0:T(8,128)S(1)}, f32[32,256]{1,0:T(8,128)}, u32[]{:S(2)}) copy-start(f32[32,256]{1,0:T(8,128)} %param.11) | copy-start | bytes 98308
  123.8 10.6 %copy-start.1 = (f32[256,16384]{1,0:T(8,128)S(1)}, f32[256,16384]{1,0:T(8,128)}, u32[]{:S(2)}) copy-start(f32[256,16384]{1,0:T(8,128)} %all-gather.2.cloned.1.call-done) | copy-start | bytes 50331652
  140.8 60.5 %all-to-all-start = ((f32[16,1,8192]{2,1,0:T(1,128)}), f32[16,1,8192]{2,1,0:T(1,128)S(1)}, u32[]{:S(2)}, u32[]{:S(2)}) async-start(f32[16,1,8192]{2,1,0:T(1,128)} %broadcast_in_dim.68), calls=%async_computation | async-start | bytes 1048576 | tf_op jit(solution)/shard_map/all_to_all | solution.py:34
  198.4 49.0 %copy-start.5 = (s32[160,2]{0,1:T(2,128)S(1)}, s32[160,2]{0,1:T(2,128)}, u32[]{:S(2)}) copy-start(s32[160,2]{0,1:T(2,128)} %param.14) | copy-start | bytes 3844
  241.7 17.0 %all-to-all-start.4 = ((f32[16,1,8192]{2,1,0:T(1,128)}), f32[16,1,8192]{2,1,0:T(1,128)S(1)}, u32[]{:S(2)}, u32[]{:S(2)}) async-start(f32[16,1,8192]{2,1,0:T(1,128)} %broadcast_in_dim.72), calls=%async_computation.4 | async-start | bytes 1048576 | tf_op jit(solution)/shard_map/all_to_all | solution.py:34
  260.1 8.2 %all-to-all-start.5 = ((f32[8,1,32]{2,1,0:T(1,128)}), f32[8,1,32]{2,1,0:T(1,128)S(1)}, u32[]{:S(2)}, u32[]{:S(2)}) async-start(f32[8,1,32]{2,1,0:T(1,128)} %broadcast_in_dim.73), calls=%async_computation.5 | async-start | bytes 8192 | tf_op jit(solution)/shard_map/all_to_all | solution.py:34
  263.4 207.7 %reduce-scatter.2.cloned.1.call-start = ((), (), s32[]{:S(2)}) async-start(), calls=%async_computation.10 | async-start | bytes 8912896 | tf_op jit(solution)/shard_map/reduce_scatter | solution.py:140
  271.1 9.2 %copy-start = (f32[256,8192]{1,0:T(8,128)S(1)}, f32[256,8192]{1,0:T(8,128)}, u32[]{:S(2)}) copy-start(f32[256,8192]{1,0:T(8,128)} %get-tuple-element.271) | copy-start | bytes 25165828 | tf_op jit(solution)/shard_map/while
  290.1 11.5 %copy-start = (f32[256,8192]{1,0:T(8,128)S(1)}, f32[256,8192]{1,0:T(8,128)}, u32[]{:S(2)}) copy-start(f32[256,8192]{1,0:T(8,128)} %get-tuple-element.271) | copy-start | bytes 25165828 | tf_op jit(solution)/shard_map/while
  311.5 11.5 %copy-start = (f32[256,8192]{1,0:T(8,128)S(1)}, f32[256,8192]{1,0:T(8,128)}, u32[]{:S(2)}) copy-start(f32[256,8192]{1,0:T(8,128)} %get-tuple-element.271) | copy-start | bytes 25165828 | tf_op jit(solution)/shard_map/while
  332.9 11.5 %copy-start = (f32[256,8192]{1,0:T(8,128)S(1)}, f32[256,8192]{1,0:T(8,128)}, u32[]{:S(2)}) copy-start(f32[256,8192]{1,0:T(8,128)} %get-tuple-element.271) | copy-start | bytes 25165828 | tf_op jit(solution)/shard_map/while
  354.3 11.5 %copy-start = (f32[256,8192]{1,0:T(8,128)S(1)}, f32[256,8192]{1,0:T(8,128)}, u32[]{:S(2)}) copy-start(f32[256,8192]{1,0:T(8,128)} %get-tuple-element.271) | copy-start | bytes 25165828 | tf_op jit(solution)/shard_map/while
  373.2 107.2 %copy-start.2 = (f32[160,256]{1,0:T(8,128)S(1)}, f32[160,256]{1,0:T(8,128)}, u32[]{:S(2)}) copy-start(f32[160,256]{1,0:T(8,128)} %param.10) | copy-start | bytes 491524
  374.5 98.0 %all-to-all-start.7 = ((f32[8,160,256]{2,1,0:T(8,128)}), f32[8,160,256]{2,1,0:T(8,128)S(1)}, u32[]{:S(2)}, u32[]{:S(2)}) async-start(f32[8,160,256]{2,1,0:T(8,128)} %broadcast_in_dim.75), calls=%async_computation.8 | async-start | bytes 2621440 | tf_op jit(solution)/shard_map/all_to_all | solution.py:34
  471.1 26.8 %copy-start.3 = (f32[16,8192]{1,0:T(8,128)S(1)}, f32[16,8192]{1,0:T(8,128)}, u32[]{:S(2)}) copy-start(f32[16,8192]{1,0:T(8,128)} %reduce-scatter.2.cloned.1.call-done) | copy-start | bytes 1572868
  474.4 22.8 %all-to-all-start.6 = ((f32[16,1,16384]{2,1,0:T(1,128)}), f32[16,1,16384]{2,1,0:T(1,128)S(1)}, u32[]{:S(2)}, u32[]{:S(2)}) async-start(f32[16,1,16384]{2,1,0:T(1,128)} %broadcast_in_dim.74), calls=%async_computation.7 | async-start | bytes 2097152 | tf_op jit(solution)/shard_map/all_to_all | solution.py:34
Sparse Core Ops, SparseCore 0:
  10.4 113.3 all-gather.1
  373.4 97.6 reduce-scatter.1
where the time goes:
time: 509 us; the launch traced here: 507 us
  waiting for transfers between devices  235 us (46%)
  matrix products  155 us (30%)
  blocking collectives  36.6 us (7%)
  other arithmetic  32 us (6%)
  starting transfers between devices  22.4 us (4%)
  between operations  15 us (3%)
  local copies, waits for them, and re-layouts  10.9 us (2%)
    all_gather x1, waiting for transfers between devices, side_by_side(): result, at, outs = (lax.all_gather(both, axis, axis=dim, tiled=True), 0, [])  111 us
    reduce_scatter x1, waiting for transfers between devices, body(): lax.psum_scatter(grad_unit, 'dp', scatter_dimension=0, tiled=True)  92.7 us
    dot_general x5, matrix products, grad_block(): jnp.dot(rows.T, dscore, precision=highest, preferred_element_type=jnp.flo...  55.2 us
    dot_general x5, matrix products, block_expo(): jnp.dot(rows, student_unit, precision=highest, preferred_element_type=jnp...  46.2 us
    dot_general x5, matrix products, grad_block(): jnp.dot(dscore, student_unit.T, precision=highest, preferred_element_type...  37 us
    all_to_all x3, blocking collectives, from_everyone(): return lax.all_to_all(copies, axis, split_axis=0, concat_axis=0, tiled=True)  36.6 us
    all_to_all x5, waiting for transfers between devices, from_everyone(): return lax.all_to_all(copies, axis, split_axis=0, concat_axis=0, tiled=True)  31.4 us
    all_to_all x5, starting transfers between devices, from_everyone(): return lax.all_to_all(copies, axis, split_axis=0, concat_axis=0, tiled=True)  22.3 us
  transfers between devices with their start and end apart: 7, of which 5 were waited for; matrix products, arithmetic and copies ran while one was open for 13% of the time, Pallas kernels for 0%

commit v1 on v0

v1 whole, which is shorter than its diff:
```python
import jax
import jax.numpy as jnp
from jax import lax
from jax.sharding import Mesh, PartitionSpec as P

CROPS = 10
GLOBAL_CROPS = 2
ITERS = 3
WARM_STEPS = 12500
TOTAL_STEPS = 625000

student_temp = 0.1
loss_scale = 16777216.0
norm_eps = 1e-06
square_eps = 1e-06
rate_peak = 0.05
weight_decay = 0.04
momentum_base = 0.994
highest = lax.Precision.HIGHEST
high = lax.Precision.HIGH
f32 = jnp.float32

AXES = ("x", "zh", "c", "y", "zl")
DP = ("x", "zh", "c")
PROTO = ("y", "zl")
CHIPS = ("x", "zh", "y", "zl")


def dot(a, b, dims, precision=high):
    return lax.dot_general(a, b, (dims, ((), ())), precision=precision, preferred_element_type=f32)


def plan(step):
    value = step[0].astype(f32)
    ramp = jnp.minimum(1.0, value / WARM_STEPS)
    rate = rate_peak * (0.25 + 0.75 * ramp)
    teacher_temp = 0.04 + 0.03 * ramp
    momentum = 1.0 - (1.0 - momentum_base) * (jnp.cos(jnp.pi * value / TOTAL_STEPS) + 1.0) * 0.5
    return (rate, teacher_temp, momentum)


def unit_rows(values):
    norm = jnp.sqrt(jnp.sum(values * values, axis=1, keepdims=True) + norm_eps)
    return (values / norm, norm)


def unit_columns(values):
    norm = jnp.sqrt(jnp.sum(values * values, axis=0, keepdims=True) + norm_eps)
    return (values / norm, norm)


def other_core(v):
    return lax.ppermute(v, "c", ((0, 1), (1, 0)))


def from_everyone(v, axes):
    n = lax.axis_size(axes)
    copies = jnp.broadcast_to(v, (n, *v.shape))
    return lax.all_to_all(copies, axes, split_axis=0, concat_axis=0, tiled=True)


def everywhere(v):
    v = v + other_core(v)
    return jnp.sum(from_everyone(v, CHIPS), axis=0)


def shifted(v, axis, by):
    n = lax.axis_size(axis)
    return lax.ppermute(v, axis, [(i, (i + by) % n) for i in range(n)])


def staged(v):
    for axis in ("x", "y", ("zh", "zl")):
        v = v + shifted(v, axis, 1) + shifted(v, axis, 3) + shifted(v, axis, 2)
    return v + other_core(v)


def body(student_feats, teacher_feats, student_proto, teacher_proto, crops, step):
    rate, teacher_temp, momentum = plan(step)
    n_dp = lax.axis_size(DP)
    n_proto = lax.axis_size(PROTO)
    own_rows, own_cols = student_proto.shape
    cols = own_cols // n_dp
    width = own_rows * n_dp
    crop_rows = student_feats.shape[0]
    teach_rows = teacher_feats.shape[0]
    images = teach_rows // GLOBAL_CROPS

    t_unit, _ = unit_rows(teacher_feats)
    s_unit, s_norm = unit_rows(student_feats)
    place = crops[:, 1] * images + crops[:, 0]
    q_iota = lax.broadcasted_iota(jnp.int32, (crop_rows, crop_rows), 0)
    sort = (q_iota == place[None, :]).astype(f32)
    s_sorted = dot(sort, s_unit, ((1,), (0,)), highest)

    def exchange(proto, rows):
        pieces = proto.reshape(own_rows, n_dp, cols).transpose(1, 0, 2)
        both = jnp.concatenate(
            [pieces, jnp.broadcast_to(rows, (n_dp, *rows.shape))], axis=1
        )
        got = lax.all_to_all(both, DP, split_axis=0, concat_axis=0, tiled=True)
        return got[:, :own_rows].reshape(width, cols), got[:, own_rows:]

    teach, t_all = exchange(teacher_proto, t_unit.reshape(images, GLOBAL_CROPS * width))
    student, s_all = exchange(student_proto, s_sorted.reshape(crop_rows // 2, 2 * width))

    teacher_unit, _ = unit_columns(teach)
    t_rows = jnp.concatenate([t_all[:, :, :width], t_all[:, :, width:]], axis=0).reshape(
        GLOBAL_CROPS * n_dp * images, width
    )
    kernel = jnp.exp(dot(t_rows, teacher_unit, ((1,), (0,))) / teacher_temp)
    row = None
    for turn in range(ITERS):
        if row is None:
            col = 1.0 / jnp.sum(kernel, axis=0)
        else:
            col = 1.0 / jnp.sum(kernel * row[:, None], axis=0)
        if turn == ITERS - 1:
            last = kernel * col[None, :]
            part = jnp.sum(last, axis=1)
        else:
            part = jnp.sum(kernel * col[None, :], axis=1)
        row = 1.0 / everywhere(part)

    student_unit, student_norm = unit_columns(student)
    s_rows = s_all.reshape(n_dp * crop_rows, width)
    expo = jnp.exp(dot(s_rows, student_unit, ((1,), (0,))) / student_temp)
    total = staged(jnp.sum(expo, axis=1).reshape(-1, 128)).reshape(n_dp, CROPS, images)
    pair_total = GLOBAL_CROPS * (GLOBAL_CROPS - 1) + (CROPS - GLOBAL_CROPS) * GLOBAL_CROPS
    coef = loss_scale / (pair_total * images * n_dp * student_temp)
    slots = lax.broadcasted_iota(jnp.int32, (1, CROPS, 1), 1)
    count = jnp.where(slots < GLOBAL_CROPS, GLOBAL_CROPS - 1.0, GLOBAL_CROPS * 1.0)
    scale = coef * count / total

    back_s = dot(expo, student_unit, ((1,), (1,))).reshape(n_dp, crop_rows, width)
    back_t = dot(last, student_unit, ((1,), (1,))).reshape(GLOBAL_CROPS, n_dp, images, width)
    back_t = back_t.transpose(1, 0, 2, 3).reshape(n_dp, teach_rows, width)

    def scattered(v):
        mine = jnp.sum(lax.all_to_all(v, DP, split_axis=0, concat_axis=0, tiled=True), axis=0)
        return jnp.sum(from_everyone(mine, PROTO), axis=0)

    mine_s = scattered(back_s)
    mine_t = scattered(back_t)
    me = lax.axis_index(DP)
    my_scale = lax.dynamic_index_in_dim(scale, me, 0, keepdims=False)
    row_blocks = row.reshape(GLOBAL_CROPS, n_dp, images)
    my_row = lax.dynamic_index_in_dim(row_blocks, me, 1, keepdims=False)
    part_t = coef * my_row[:, :, None] * mine_t.reshape(GLOBAL_CROPS, images, width)
    both_t = part_t[0] + part_t[1]
    target = jnp.concatenate(
        [part_t[1][None], part_t[0][None], jnp.broadcast_to(both_t, (CROPS - GLOBAL_CROPS, *both_t.shape))]
    ).reshape(crop_rows, width)
    feature_sorted = mine_s * my_scale.reshape(crop_rows, 1) - target
    feature_unit = dot(sort, feature_sorted, ((0,), (0,)), highest)
    feature_grad = (
        feature_unit - s_unit * jnp.sum(s_unit * feature_unit, axis=1, keepdims=True)
    ) / s_norm

    scaled = s_rows * scale.reshape(-1, 1)
    grad_s = dot(scaled, expo, ((0,), (0,)))
    by_slot = s_all.reshape(n_dp, CROPS, images, width)
    local = jnp.sum(by_slot[:, GLOBAL_CROPS:], axis=1)
    weights = jnp.stack([by_slot[:, 1] + local, by_slot[:, 0] + local]).reshape(-1, width)
    grad_t = dot(weights * (coef * row)[:, None], last, ((0,), (0,)))
    grad = grad_s - grad_t
    along = jnp.sum(student_unit * grad, axis=0, keepdims=True)
    proto_grad = (grad - student_unit * along) / student_norm
    square = jnp.mean(proto_grad * proto_grad, axis=0, keepdims=True)
    direction = proto_grad / jnp.sqrt(square + square_eps)
    next_cols = student - rate * (direction + weight_decay * student)
    back = lax.all_to_all(
        next_cols.reshape(n_dp, own_rows, cols), DP, split_axis=0, concat_axis=0, tiled=True
    )
    student_next = back.transpose(1, 0, 2).reshape(own_rows, own_cols)
    teacher_next = momentum * teacher_proto + (1.0 - momentum) * student_next
    return (student_next, teacher_next, feature_grad)


def solution(mesh):
    n_x, n_zh, n_c, n_y, n_zl = 4, 2, 2, 4, 2
    fine = Mesh(mesh.devices.reshape(n_x, n_zh, n_c, n_y, n_zl), AXES)
    in_specs = (P(DP, None), P(DP, None), P(DP, PROTO), P(DP, PROTO), P(DP, None), P())
    out_specs = (P(DP, PROTO), P(DP, PROTO), P(DP, None))
    return jax.shard_map(body, mesh=fine, in_specs=in_specs, out_specs=out_specs, check_vma=False)
```

time: 509 us -> 283 us (0.56)
  matrix products: 155 us -> 16.8 us
  waiting for transfers between devices: 235 us -> 146 us
  starting transfers between devices: 22.4 us -> 76.3 us
  blocking collectives: 36.6 us -> 0 us
  other arithmetic: 32 us -> 16.5 us
  between operations: 15 us -> 1.91 us
  local copies, waits for them, and re-layouts: 10.9 us -> 19.6 us
    dot_general x21 -> x8, matrix products: 155 us -> 16.8 us  [dot(): lax.dot_general(a, b, (dims, ((), ())), precision=precision, preferred_el...]
    all_gather x1 -> x0, waiting for transfers between devices: 111 us -> none  [side_by_side(): result, at, outs = (lax.all_gather(both, axis, axis=dim, tiled=True), 0, [])]
    all_to_all x5 -> x10, waiting for transfers between devices: 31.4 us -> 138 us  [the longest x2 55.7 us: exchange(): got = lax.all_to_all(both, DP, split_axis=0, concat_axis=0, tiled=True)]
    reduce_scatter x1 -> x0, waiting for transfers between devices: 92.7 us -> none  [body(): lax.psum_scatter(grad_unit, 'dp', scatter_dimension=0, tiled=True)]
    all_to_all x3 -> x0, blocking collectives: 36.6 us -> none  [from_everyone(): return lax.all_to_all(copies, axis, split_axis=0, concat_axis=0, tiled=True)]
    all_to_all x5 -> x10, starting transfers between devices: 22.3 us -> 58.2 us  [the longest x5 23 us: from_everyone(): return lax.all_to_all(copies, axes, split_axis=0, concat_axis=0, tiled=True)]
    ppermute x0 -> x13, starting transfers between devices: none -> 18.1 us  [the longest x9 10 us: shifted(): return lax.ppermute(v, axis, [(i, (i + by) % n) for i in range(n)])]
    ppermute x0 -> x13, waiting for transfers between devices: none -> 8.24 us  [the longest x9 6.16 us: shifted(): return lax.ppermute(v, axis, [(i, (i + by) % n) for i in range(n)])]
  transfers between devices with their start and end apart: 7 -> 23, of which waited for: 5 -> 17; matrix products, arithmetic and copies ran while one was open for 13% -> 8% of each run, Pallas kernels for 0% -> 0%
where the time goes in v1:
time: 283 us; the launch traced here: 277 us
  waiting for transfers between devices  146 us (52%)
  starting transfers between devices  76.3 us (27%)
  local copies, waits for them, and re-layouts  19.6 us (7%)
  matrix products  16.8 us (6%)
  other arithmetic  16.5 us (6%)
    all_to_all x2, waiting for transfers between devices, exchange(): got = lax.all_to_all(both, DP, split_axis=0, concat_axis=0, tiled=True)  55.7 us
    all_to_all x5, waiting for transfers between devices, from_everyone(): return lax.all_to_all(copies, axes, split_axis=0, concat_axis=0, tiled=True)  43.4 us
    all_to_all x2, waiting for transfers between devices, scattered(): lax.all_to_all(v, DP, split_axis=0, concat_axis=0, tiled=True)  33.8 us
    all_to_all x5, starting transfers between devices, from_everyone(): return lax.all_to_all(copies, axes, split_axis=0, concat_axis=0, tiled=True)  23 us
    dot_general x8, matrix products, dot(): lax.dot_general(a, b, (dims, ((), ())), precision=precision, preferred_el...  16.8 us
    all_to_all x2, starting transfers between devices, exchange(): got = lax.all_to_all(both, DP, split_axis=0, concat_axis=0, tiled=True)  15.1 us
    all_to_all x2, starting transfers between devices, scattered(): lax.all_to_all(v, DP, split_axis=0, concat_axis=0, tiled=True)  14.9 us
    ppermute x9, starting transfers between devices, shifted(): return lax.ppermute(v, axis, [(i, (i + by) % n) for i in range(n)])  10 us
  transfers between devices with their start and end apart: 23, of which 17 were waited for; matrix products, arithmetic and copies ran while one was open for 8% of the time, Pallas kernels for 0%

profile of v1, /device:TPU:1, one launch (start us, length us, event | category | flops | bytes accessed | tf_op | source)
XLA Modules:
  0.0 277.3 jit_solution(14871995704815807387)
XLA Ops:
  5.5 9.1 %all-to-all-start.1 = ((f32[16,32,512]{2,1,0:T(8,128)}), f32[16,32,512]{2,1,0:T(8,128)S(1)}, u32[]{:S(2)}, u32[]{:S(2)}) async-start(f32[16,32,512]{2,1,0:T(8,128)} %copy.34), calls=%async_computation.1 | async-start | bytes 2097152 | tf_op jit(solution)/shard_map/all_to_all | solution.py:101
  15.3 16.3 %all-to-all-done.1 = f32[16,32,512]{2,1,0:T(8,128)S(1)} async-done(((f32[16,32,512]{2,1,0:T(8,128)}), f32[16,32,512]{2,1,0:T(8,128)S(1)}, u32[]{:S(2)}, u32[]{:S(2)}) %all-to-all-start.1) | async-done | bytes 1048608 | tf_op jit(solution)/shard_map/all_to_all | solution.py:101
  35.4 6.7 %all-to-all-start.2 = ((f32[64,1,512]{2,1,0:T(1,128)}), f32[64,1,512]{2,1,0:T(1,128)S(1)}, u32[]{:S(2)}, u32[]{:S(2)}) async-start(f32[64,1,512]{2,1,0:T(1,128)} %broadcast_in_dim.51), calls=%async_computation.2 | async-start | bytes 262144 | tf_op jit(solution)/shard_map/all_to_all | solution.py:59
  42.2 8.7 %all-to-all-done.2 = f32[64,1,512]{2,1,0:T(1,128)S(1)} async-done(((f32[64,1,512]{2,1,0:T(1,128)}), f32[64,1,512]{2,1,0:T(1,128)S(1)}, u32[]{:S(2)}, u32[]{:S(2)}) %all-to-all-start.2) | async-done | bytes 131104 | tf_op jit(solution)/shard_map/all_to_all | solution.py:59
  54.6 4.6 %all-to-all-start.3 = ((f32[64,1,512]{2,1,0:T(1,128)}), f32[64,1,512]{2,1,0:T(1,128)S(1)}, u32[]{:S(2)}, u32[]{:S(2)}) async-start(f32[64,1,512]{2,1,0:T(1,128)} %broadcast_in_dim.52), calls=%async_computation.3 | async-start | bytes 262144 | tf_op jit(solution)/shard_map/all_to_all | solution.py:59
  59.2 8.7 %all-to-all-done.3 = f32[64,1,512]{2,1,0:T(1,128)S(1)} async-done(((f32[64,1,512]{2,1,0:T(1,128)}), f32[64,1,512]{2,1,0:T(1,128)S(1)}, u32[]{:S(2)}, u32[]{:S(2)}) %all-to-all-start.3) | async-done | bytes 131104 | tf_op jit(solution)/shard_map/all_to_all | solution.py:59
  72.5 4.6 %all-to-all-start.4 = ((f32[64,1,512]{2,1,0:T(1,128)}), f32[64,1,512]{2,1,0:T(1,128)S(1)}, u32[]{:S(2)}, u32[]{:S(2)}) async-start(f32[64,1,512]{2,1,0:T(1,128)} %broadcast_in_dim.53), calls=%async_computation.4 | async-start | bytes 262144 | tf_op jit(solution)/shard_map/all_to_all | solution.py:59
  77.5 2.1 pad_maximum_fusion
  79.6 6.3 %all-to-all-done.4 = f32[64,1,512]{2,1,0:T(1,128)S(1)} async-done(((f32[64,1,512]{2,1,0:T(1,128)}), f32[64,1,512]{2,1,0:T(1,128)S(1)}, u32[]{:S(2)}, u32[]{:S(2)}) %all-to-all-start.4) | async-done | bytes 131104 | tf_op jit(solution)/shard_map/all_to_all | solution.py:59
  85.8 5.9 %all-to-all-start = ((f32[16,96,512]{2,1,0:T(8,128)}), f32[16,96,512]{2,1,0:T(8,128)}, u32[]{:S(2)}, u32[]{:S(2)}) async-start(f32[16,96,512]{2,1,0:T(8,128)} %pad_maximum_fusion), calls=%async_computation | async-start | bytes 6291456 | tf_op jit(solution)/shard_map/all_to_all | solution.py:101
  92.1 39.4 %all-to-all-done = f32[16,96,512]{2,1,0:T(8,128)} async-done(((f32[16,96,512]{2,1,0:T(8,128)}), f32[16,96,512]{2,1,0:T(8,128)}, u32[]{:S(2)}, u32[]{:S(2)}) %all-to-all-start) | async-done | bytes 3145760 | tf_op jit(solution)/shard_map/all_to_all | solution.py:101
  131.5 2.1 slice.54
  136.9 2.6 reshape.247
  142.2 5.0 %fusion.20 = (f32[2560]{0:T(1024)S(1)}, f32[2560,512]{1,0:T(8,128)}) fusion(f32[2560,256]{1,0:T(8,128)S(1)} %reshape.247, f32[256,512]{1,0:T(8,128)S(1)} %bitcast.92), kind=kOutput, calls=%fused_computation.77 | convolution fusion | flops 2015884800 | bytes 8398848 | tf_op jit(solution)/shard_map/dot_general | solution.py:30
  147.2 2.4 collective-permute-start.1
  151.8 10.1 %all-to-all-start.8 = ((f32[16,32,256]{2,1,0:T(8,128)}), f32[16,32,256]{2,1,0:T(8,128)S(1)}, u32[]{:S(2)}, u32[]{:S(2)}) async-start(f32[16,32,256]{2,1,0:T(8,128)} %bitcast.25), calls=%async_computation.8 | async-start | bytes 1048576 | tf_op jit(solution)/shard_map/all_to_all | solution.py:140
  162.0 2.0 slice_reduce_fusion
  166.3 1.8 collective-permute-start.4
  169.8 2.4 collective-permute-done.3
  172.2 2.6 collective-permute-start.8
  178.5 3.5 %collective-permute-start.9 = (f32[20,128]{1,0:T(8,128)S(1)}, f32[20,128]{1,0:T(8,128)S(1)}, u32[]{:S(2)}, u32[]{:S(2)}) collective-permute-start(f32[20,128]{1,0:T(8,128)S(1)} %add_add_fusion), channel_id=1, source_target_pairs={{0,8},{8,0},{1,9},{9,1},{2,10},{10,2},{3,11},{11,3},{4,12},{12,4},... | collective-permute-start | bytes 30728 | tf_op jit(solution)/shard_map/ppermute | solution.py:53
  182.9 2.9 %multiply_reduce_fusion.5 = (f32[512]{0:T(512)S(1)}, f32[256,512]{1,0:T(8,128)S(1)}) fusion(f32[512]{0:T(512)S(1)} %add_sqrt_fusion.1, f32[16,16,512]{2,1,0:T(8,128)S(1)} %get-tuple-element.10, f32[256,512]{1,0:T(8,128)S(1)} %fusion.21, f32[2560,512]{1,0:T(8,128)S(1)} %bitcast.90, f32[2560,256]{1,0:T(8,128)S(1)} %copy-done.1, f32[2560]{0:T(1024)S(1)} %get-tuple-element.3), kind=kOutput, calls=%fused_computation.27 | convolution fusion | flops 2014445056 | bytes 9451520 | tf_op jit(solution)/shard_map/dot_general | solution.py:30
  186.9 5.3 %all-to-all-start.5 = ((f32[16,16,512]{2,1,0:T(8,128)}), f32[16,16,512]{2,1,0:T(8,128)S(1)}, u32[]{:S(2)}, u32[]{:S(2)}) async-start(f32[16,16,512]{2,1,0:T(8,128)} %bitcast.15), calls=%async_computation.5 | async-start | bytes 1048576 | tf_op jit(solution)/shard_map/all_to_all | solution.py:172
  192.2 6.2 %fusion.22 = f32[16,160,256]{2,1,0:T(8,128)} fusion(f32[16,160,512]{2,1,0:T(8,128)} %bitcast.88, f32[256,512,1]{1,0,2:T(8,128)S(1)} %bitcast.94), kind=kOutput, calls=%fused_computation.79 | convolution fusion | flops 2013265920 | bytes 8388608 | tf_op jit(solution)/shard_map/dot_general | solution.py:30
  198.5 5.0 %all-to-all-done.5 = f32[16,16,512]{2,1,0:T(8,128)S(1)} async-done(((f32[16,16,512]{2,1,0:T(8,128)}), f32[16,16,512]{2,1,0:T(8,128)S(1)}, u32[]{:S(2)}, u32[]{:S(2)}) %all-to-all-start.5) | async-done | bytes 524320 | tf_op jit(solution)/shard_map/all_to_all | solution.py:172
  204.2 4.7 %all-to-all-start.6 = ((f32[16,160,256]{2,1,0:T(8,128)}), f32[16,160,256]{2,1,0:T(8,128)S(1)}, u32[]{:S(2)}, u32[]{:S(2)}) async-start(f32[16,160,256]{2,1,0:T(8,128)} %fusion.22), calls=%async_computation.6 | async-start | bytes 5242880 | tf_op jit(solution)/shard_map/all_to_all | solution.py:140
  209.2 33.8 %all-to-all-done.6 = f32[16,160,256]{2,1,0:T(8,128)S(1)} async-done(((f32[16,160,256]{2,1,0:T(8,128)}), f32[16,160,256]{2,1,0:T(8,128)S(1)}, u32[]{:S(2)}, u32[]{:S(2)}) %all-to-all-start.6) | async-done | bytes 2621472 | tf_op jit(solution)/shard_map/all_to_all | solution.py:140
  243.7 3.4 %all-to-all-start.9 = ((f32[8,32,256]{2,1,0:T(8,128)}), f32[8,32,256]{2,1,0:T(8,128)S(1)}, u32[]{:S(2)}, u32[]{:S(2)}) async-start(f32[8,32,256]{2,1,0:T(8,128)} %broadcast_in_dim.55), calls=%async_computation.9 | async-start | bytes 524288 | tf_op jit(solution)/shard_map/all_to_all | solution.py:59
  249.4 3.6 %all-to-all-done.9 = f32[8,32,256]{2,1,0:T(8,128)S(1)} async-done(((f32[8,32,256]{2,1,0:T(8,128)}), f32[8,32,256]{2,1,0:T(8,128)S(1)}, u32[]{:S(2)}, u32[]{:S(2)}) %all-to-all-start.9) | async-done | bytes 262176 | tf_op jit(solution)/shard_map/all_to_all | solution.py:59
  253.0 2.1 broadcast_in_dim.54
  255.0 3.6 %all-to-all-start.7 = ((f32[8,160,256]{2,1,0:T(8,128)}), f32[8,160,256]{2,1,0:T(8,128)S(1)}, u32[]{:S(2)}, u32[]{:S(2)}) async-start(f32[8,160,256]{2,1,0:T(8,128)} %broadcast_in_dim.54), calls=%async_computation.7 | async-start | bytes 2621440 | tf_op jit(solution)/shard_map/all_to_all | solution.py:59
  259.6 16.2 %all-to-all-done.7 = f32[8,160,256]{2,1,0:T(8,128)S(1)} async-done(((f32[8,160,256]{2,1,0:T(8,128)}), f32[8,160,256]{2,1,0:T(8,128)S(1)}, u32[]{:S(2)}, u32[]{:S(2)}) %all-to-all-start.7) | async-done | bytes 1310752 | tf_op jit(solution)/shard_map/all_to_all | solution.py:59
  (139 shorter events, 41.6 us)
Async XLA Ops:
  5.5 26.1 %all-to-all-start.1 = ((f32[16,32,512]{2,1,0:T(8,128)}), f32[16,32,512]{2,1,0:T(8,128)S(1)}, u32[]{:S(2)}, u32[]{:S(2)}) async-start(f32[16,32,512]{2,1,0:T(8,128)} %copy.34), calls=%async_computation.1 | async-start | bytes 2097152 | tf_op jit(solution)/shard_map/all_to_all | solution.py:101
  31.8 10.4 %copy-start.15 = (s32[160,2]{0,1:T(2,128)S(1)}, s32[160,2]{0,1:T(2,128)}, u32[]{:S(2)}) copy-start(s32[160,2]{0,1:T(2,128)} %param.10) | copy-start | bytes 3844
  32.5 20.5 %copy-start.12 = (f32[160,256]{1,0:T(8,128)S(1)}, f32[160,256]{1,0:T(8,128)}, u32[]{:S(2)}) copy-start(f32[160,256]{1,0:T(8,128)} %param.6) | copy-start | bytes 491524
  32.7 2.0 collective-permute-start.10
  35.4 15.5 %all-to-all-start.2 = ((f32[64,1,512]{2,1,0:T(1,128)}), f32[64,1,512]{2,1,0:T(1,128)S(1)}, u32[]{:S(2)}, u32[]{:S(2)}) async-start(f32[64,1,512]{2,1,0:T(1,128)} %broadcast_in_dim.51), calls=%async_computation.2 | async-start | bytes 262144 | tf_op jit(solution)/shard_map/all_to_all | solution.py:59
  51.3 20.0 %copy-start.14 = (f32[16,8192]{1,0:T(8,128)S(1)}, f32[16,8192]{1,0:T(8,128)}, u32[]{:S(2)}) copy-start(f32[16,8192]{1,0:T(8,128)} %param.8) | copy-start | bytes 1572868
  51.3 2.5 collective-permute-start.11
  54.6 13.3 %all-to-all-start.3 = ((f32[64,1,512]{2,1,0:T(1,128)}), f32[64,1,512]{2,1,0:T(1,128)S(1)}, u32[]{:S(2)}, u32[]{:S(2)}) async-start(f32[64,1,512]{2,1,0:T(1,128)} %broadcast_in_dim.52), calls=%async_computation.3 | async-start | bytes 262144 | tf_op jit(solution)/shard_map/all_to_all | solution.py:59
  69.2 2.5 collective-permute-start.12
  72.5 13.3 %all-to-all-start.4 = ((f32[64,1,512]{2,1,0:T(1,128)}), f32[64,1,512]{2,1,0:T(1,128)S(1)}, u32[]{:S(2)}, u32[]{:S(2)}) async-start(f32[64,1,512]{2,1,0:T(1,128)} %broadcast_in_dim.53), calls=%async_computation.4 | async-start | bytes 262144 | tf_op jit(solution)/shard_map/all_to_all | solution.py:59
  85.8 45.7 %all-to-all-start = ((f32[16,96,512]{2,1,0:T(8,128)}), f32[16,96,512]{2,1,0:T(8,128)}, u32[]{:S(2)}, u32[]{:S(2)}) async-start(f32[16,96,512]{2,1,0:T(8,128)} %pad_maximum_fusion), calls=%async_computation | async-start | bytes 6291456 | tf_op jit(solution)/shard_map/all_to_all | solution.py:101
  147.2 18.1 %collective-permute-start.1 = (f32[20,128]{1,0:T(8,128)S(1)}, f32[20,128]{1,0:T(8,128)S(1)}, u32[]{:S(2)}, u32[]{:S(2)}) collective-permute-start(f32[20,128]{1,0:T(8,128)S(1)} %bitcast.105), channel_id=1, source_target_pairs={{0,96},{32,0},{64,32},{96,64},{1,97},{33,1},{65,33},{97,65},{2,98}... | collective-permute-start | bytes 30728 | tf_op jit(solution)/shard_map/ppermute | solution.py:69
  149.6 15.7 %collective-permute-start.2 = (f32[20,128]{1,0:T(8,128)S(1)}, f32[20,128]{1,0:T(8,128)S(1)}, u32[]{:S(2)}, u32[]{:S(2)}) collective-permute-start(f32[20,128]{1,0:T(8,128)S(1)} %bitcast.106), channel_id=1, source_target_pairs={{0,64},{32,96},{64,0},{96,32},{1,65},{33,97},{65,1},{97,33},{2,66}... | collective-permute-start | bytes 30728 | tf_op jit(solution)/shard_map/ppermute | solution.py:69
  149.6 15.7 %collective-permute-start = (f32[20,128]{1,0:T(8,128)S(1)}, f32[20,128]{1,0:T(8,128)S(1)}, u32[]{:S(2)}, u32[]{:S(2)}) collective-permute-start(f32[20,128]{1,0:T(8,128)S(1)} %bitcast.107), channel_id=1, source_target_pairs={{0,32},{32,64},{64,96},{96,0},{1,33},{33,65},{65,97},{97,1},{2,34}... | collective-permute-start | bytes 30728 | tf_op jit(solution)/shard_map/ppermute | solution.py:69
  150.4 32.5 %slice-start = ((s8[5242880]{0:T(1024)(128)(4,1)}), s8[1048576]{0:T(1024)(128)(4,1)S(1)}, s32[]{:S(2)}) async-start(s8[5242880]{0:T(1024)(128)(4,1)} %bitcast.89), calls=%async_computation.10 | async-start | bytes 2097152
  151.8 35.1 %all-to-all-start.8 = ((f32[16,32,256]{2,1,0:T(8,128)}), f32[16,32,256]{2,1,0:T(8,128)S(1)}, u32[]{:S(2)}, u32[]{:S(2)}) async-start(f32[16,32,256]{2,1,0:T(8,128)} %bitcast.25), calls=%async_computation.8 | async-start | bytes 1048576 | tf_op jit(solution)/shard_map/all_to_all | solution.py:140
  162.0 20.1 %copy-start.4 = (f32[512,512]{1,0:T(8,128)S(1)}, f32[512,512]{1,0:T(8,128)}, u32[]{:S(2)}) copy-start(f32[512,512]{1,0:T(8,128)} %get-tuple-element.8) | copy-start | bytes 3145732
  162.0 20.9 %slice-start.1 = ((s8[5242880]{0:T(1024)(128)(4,1)}), s8[4194304]{0:T(1024)(128)(4,1)S(1)}, s32[]{:S(2)}) async-start(s8[5242880]{0:T(1024)(128)(4,1)} %bitcast.89), calls=%async_computation.11 | async-start | bytes 8388608
  164.0 18.9 %copy-start.1 = (f32[2560,256]{1,0:T(8,128)S(1)}, f32[2560,256]{1,0:T(8,128)}, u32[]{:S(2)}) copy-start(f32[2560,256]{1,0:T(8,128)} %copy-done) | copy-start | bytes 7864324
  165.3 4.4 %collective-permute-start.5 = (f32[20,128]{1,0:T(8,128)S(1)}, f32[20,128]{1,0:T(8,128)S(1)}, u32[]{:S(2)}, u32[]{:S(2)}) collective-permute-start(f32[20,128]{1,0:T(8,128)S(1)} %add_add_fusion.2), channel_id=1, source_target_pairs={{0,4},{2,6},{4,0},{6,2},{1,5},{3,7},{5,1},{7,3},{8,12},{10,14},{12... | collective-permute-start | bytes 30728 | tf_op jit(solution)/shard_map/ppermute | solution.py:69
  166.3 3.5 %collective-permute-start.4 = (f32[20,128]{1,0:T(8,128)S(1)}, f32[20,128]{1,0:T(8,128)S(1)}, u32[]{:S(2)}, u32[]{:S(2)}) collective-permute-start(f32[20,128]{1,0:T(8,128)S(1)} %add_add_fusion.2), channel_id=1, source_target_pairs={{0,6},{2,0},{4,2},{6,4},{1,7},{3,1},{5,3},{7,5},{8,14},{10,8},{12,... | collective-permute-start | bytes 30728 | tf_op jit(solution)/shard_map/ppermute | solution.py:69
  168.1 4.1 %collective-permute-start.3 = (f32[20,128]{1,0:T(8,128)S(1)}, f32[20,128]{1,0:T(8,128)S(1)}, u32[]{:S(2)}, u32[]{:S(2)}) collective-permute-start(f32[20,128]{1,0:T(8,128)S(1)} %add_add_fusion.2), channel_id=1, source_target_pairs={{0,2},{2,4},{4,6},{6,0},{1,3},{3,5},{5,7},{7,1},{8,10},{10,12},{12... | collective-permute-start | bytes 30728 | tf_op jit(solution)/shard_map/ppermute | solution.py:69
  172.2 4.2 %collective-permute-start.8 = (f32[20,128]{1,0:T(8,128)S(1)}, f32[20,128]{1,0:T(8,128)S(1)}, u32[]{:S(2)}, u32[]{:S(2)}) collective-permute-start(f32[20,128]{1,0:T(8,128)S(1)} %add_add_fusion.1), channel_id=1, source_target_pairs={{0,16},{1,17},{16,0},{17,1},{2,18},{3,19},{18,2},{19,3},{4,20},{5,... | collective-permute-start | bytes 30728 | tf_op jit(solution)/shard_map/ppermute | solution.py:69
  174.7 2.8 %collective-permute-start.7 = (f32[20,128]{1,0:T(8,128)S(1)}, f32[20,128]{1,0:T(8,128)S(1)}, u32[]{:S(2)}, u32[]{:S(2)}) collective-permute-start(f32[20,128]{1,0:T(8,128)S(1)} %add_add_fusion.1), channel_id=1, source_target_pairs={{0,17},{1,0},{16,1},{17,16},{2,19},{3,2},{18,3},{19,18},{4,21},{5,... | collective-permute-start | bytes 30728 | tf_op jit(solution)/shard_map/ppermute | solution.py:69
  174.7 3.8 %collective-permute-start.6 = (f32[20,128]{1,0:T(8,128)S(1)}, f32[20,128]{1,0:T(8,128)S(1)}, u32[]{:S(2)}, u32[]{:S(2)}) collective-permute-start(f32[20,128]{1,0:T(8,128)S(1)} %add_add_fusion.1), channel_id=1, source_target_pairs={{0,1},{1,16},{16,17},{17,0},{2,3},{3,18},{18,19},{19,2},{4,5},{5,2... | collective-permute-start | bytes 30728 | tf_op jit(solution)/shard_map/ppermute | solution.py:69
  178.5 4.4 %collective-permute-start.9 = (f32[20,128]{1,0:T(8,128)S(1)}, f32[20,128]{1,0:T(8,128)S(1)}, u32[]{:S(2)}, u32[]{:S(2)}) collective-permute-start(f32[20,128]{1,0:T(8,128)S(1)} %add_add_fusion), channel_id=1, source_target_pairs={{0,8},{8,0},{1,9},{9,1},{2,10},{10,2},{3,11},{11,3},{4,12},{12,4},... | collective-permute-start | bytes 30728 | tf_op jit(solution)/shard_map/ppermute | solution.py:53
  186.9 11.6 %copy-start.7 = (f32[16,32,256]{2,1,0:T(8,128)}, f32[16,32,256]{2,1,0:T(8,128)S(1)}, u32[]{:S(2)}) copy-start(f32[16,32,256]{2,1,0:T(8,128)S(1)} %all-to-all-done.8) | copy-start | bytes 1572868
  186.9 16.5 %all-to-all-start.5 = ((f32[16,16,512]{2,1,0:T(8,128)}), f32[16,16,512]{2,1,0:T(8,128)S(1)}, u32[]{:S(2)}, u32[]{:S(2)}) async-start(f32[16,16,512]{2,1,0:T(8,128)} %bitcast.15), calls=%async_computation.5 | async-start | bytes 1048576 | tf_op jit(solution)/shard_map/all_to_all | solution.py:172
  204.2 38.8 %all-to-all-start.6 = ((f32[16,160,256]{2,1,0:T(8,128)}), f32[16,160,256]{2,1,0:T(8,128)S(1)}, u32[]{:S(2)}, u32[]{:S(2)}) async-start(f32[16,160,256]{2,1,0:T(8,128)} %fusion.22), calls=%async_computation.6 | async-start | bytes 5242880 | tf_op jit(solution)/shard_map/all_to_all | solution.py:140
  243.7 9.3 %all-to-all-start.9 = ((f32[8,32,256]{2,1,0:T(8,128)}), f32[8,32,256]{2,1,0:T(8,128)S(1)}, u32[]{:S(2)}, u32[]{:S(2)}) async-start(f32[8,32,256]{2,1,0:T(8,128)} %broadcast_in_dim.55), calls=%async_computation.9 | async-start | bytes 524288 | tf_op jit(solution)/shard_map/all_to_all | solution.py:59
  255.0 20.8 %all-to-all-start.7 = ((f32[8,160,256]{2,1,0:T(8,128)}), f32[8,160,256]{2,1,0:T(8,128)S(1)}, u32[]{:S(2)}, u32[]{:S(2)}) async-start(f32[8,160,256]{2,1,0:T(8,128)} %broadcast_in_dim.54), calls=%async_computation.7 | async-start | bytes 2621440 | tf_op jit(solution)/shard_map/all_to_all | solution.py:59
  258.6 17.4 %copy-start.13 = (f32[160,256]{1,0:T(8,128)S(1)}, f32[160,256]{1,0:T(8,128)}, u32[]{:S(2)}) copy-start(f32[160,256]{1,0:T(8,128)} %param.6) | copy-start | bytes 491524
  (9 other events, 58.0 us)

commit v2 on v1

v2 whole, which is shorter than its diff:
```python
import functools

import jax
import jax.numpy as jnp
from jax import lax
from jax.experimental import pallas as pl
from jax.experimental.pallas import tpu as pltpu
from jax.sharding import Mesh, PartitionSpec as P

CROPS = 10
GLOBAL_CROPS = 2
WARM_STEPS = 12500
TOTAL_STEPS = 625000

student_temp = 0.1
loss_scale = 16777216.0
norm_eps = 1e-06
square_eps = 1e-06
rate_peak = 0.05
weight_decay = 0.04
momentum_base = 0.994
highest = lax.Precision.HIGHEST
high = lax.Precision.HIGH
f32 = jnp.float32
bf16 = jnp.bfloat16


AXES = ("x", "zh", "c", "y", "zl")
DP = ("x", "zh", "c")
PROTO = ("y", "zl")
CHIPS = ("x", "zh", "y", "zl")


def dot(a, b, dims, precision=high):
    return lax.dot_general(a, b, (dims, ((), ())), precision=precision, preferred_element_type=f32)


def plan(step):
    value = step[0].astype(f32)
    ramp = jnp.minimum(1.0, value / WARM_STEPS)
    rate = rate_peak * (0.25 + 0.75 * ramp)
    teacher_temp = 0.04 + 0.03 * ramp
    momentum = 1.0 - (1.0 - momentum_base) * (jnp.cos(jnp.pi * value / TOTAL_STEPS) + 1.0) * 0.5
    return (rate, teacher_temp, momentum)


NN = ((1,), (0,))
NT = ((1,), (1,))


def halves(v):
    high_part = v.astype(bf16)
    return high_part, (v - high_part.astype(f32)).astype(bf16)


def mul(a, b, dims):
    return lax.dot_general(a, b, (dims, ((), ())), preferred_element_type=f32)


def mul3(a, b, dims):
    return mul(a[0], b[0], dims) + mul(a[0], b[1], dims) + mul(a[1], b[0], dims)


def exact_pick(pick, v):
    one = v.astype(bf16)
    rest = v - one.astype(f32)
    two = rest.astype(bf16)
    three = (rest - two.astype(f32)).astype(bf16)
    return mul(pick, one, NN) + mul(pick, two, NN) + mul(pick, three, NN)


VMEM = pl.BlockSpec(memory_space=pltpu.VMEM)
SMEM = pl.BlockSpec(memory_space=pltpu.SMEM)
HBM = pl.BlockSpec(memory_space=pltpu.HBM)
DMA = pltpu.SemaphoreType.DMA


def shape(*dims):
    return jax.ShapeDtypeStruct(dims, f32)


def room_for(*dims):
    return pltpu.VMEM(dims, f32)


def call(kernel, ins, outs, scratch=(), room=16000):
    return pl.pallas_call(
        kernel,
        in_specs=ins,
        out_specs=[spec for spec, _ in outs],
        out_shape=[out for _, out in outs],
        scratch_shapes=list(scratch),
        compiler_params=pltpu.CompilerParams(vmem_limit_bytes=room * 1024),
    )


def begin(src, dst, sem):
    copy = pltpu.make_async_copy(src, dst, sem)
    copy.start()
    return copy


def rows_kernel(turn, place, sf, tf, out, s_v, t_v):
    t = tf[...]
    t = t / jnp.sqrt(jnp.sum(t * t, axis=1, keepdims=True) + norm_eps)
    n = t.shape[0]
    q = lax.broadcasted_iota(jnp.int32, (n, n), 0)
    r = lax.broadcasted_iota(jnp.int32, (n, n), 1)
    half = n // GLOBAL_CROPS
    t_v[...] = exact_pick((r == GLOBAL_CROPS * (q % half) + q // half).astype(bf16), t)
    s = sf[...]
    s = s / jnp.sqrt(jnp.sum(s * s, axis=1, keepdims=True) + norm_eps)
    n = s.shape[0]
    q = lax.broadcasted_iota(jnp.int32, (n, n), 0)
    s_v[...] = exact_pick((q == place[...]).astype(bf16), s)
    total = sf.shape[0] + tf.shape[0]
    few_s = sf.shape[0] * out.shape[0] // total
    few_t = out.shape[0] - few_s
    out[:few_s] = s_v[pl.ds(pl.multiple_of(turn[0] * few_s, 8), few_s)]
    out[few_s:] = t_v[pl.ds(pl.multiple_of(turn[0] * few_t, 8), few_t)]


def pieces_kernel(tp, sp, pieces, tp_v, sp_v, in_sems, out_sems):
    n_dp, _, _, cols = pieces.shape
    loads = [begin(tp, tp_v, in_sems.at[0]), begin(sp, sp_v, in_sems.at[1])]
    stores = []
    for k, src in enumerate((tp_v, sp_v)):
        loads[k].wait()
        for i in range(n_dp):
            stores.append(
                begin(src.at[:, i * cols : (i + 1) * cols], pieces.at[i, k], out_sems.at[i, k])
            )
    for copy in stores:
        copy.wait()


def assembled(turn, pieces, to, rows, skip):
    turns, blks, _, _ = pieces.shape
    few = rows // turns
    for d in range(turns):
        place = pl.multiple_of((turn[0] + d) % turns * few, 8)
        for j in range(blks):
            to(j, place, few, pieces[d, j, skip : skip + few])


def teacher_kernel(index, turn, temp, got, own, other, kt_out, part_out, t_scr):
    n_all, t_rows, width = t_scr.shape
    n_blk = n_all // 2
    skip = own.shape[2] - t_rows // own.shape[0]
    teach = got[:, 0].reshape(width, got.shape[-1])
    norm = jnp.sqrt(jnp.sum(teach * teach, axis=0, keepdims=True) + norm_eps)
    unit = (teach / norm).T
    for half, pieces in enumerate((own, other)):

        def put(j, place, few, rows):
            t_scr[index[half * n_blk + j], pl.ds(place, few)] = rows

        assembled(turn, pieces, put, t_rows, skip)
    t = t_scr[...].reshape(n_all * t_rows, width)
    kt = jnp.exp(mul3(halves(unit), halves(t), NT) / temp[0])
    kt_out[...] = kt
    col = 1.0 / jnp.sum(kt, axis=1, keepdims=True)
    part_out[...] = jnp.sum(kt * col, axis=0, keepdims=True)


def scaled_round(kt_in, got):
    kt = kt_in[...]
    row = 1.0 / jnp.sum(got[:, :, : kt.shape[1]], axis=0)
    col = 1.0 / jnp.sum(kt * row, axis=1, keepdims=True)
    return kt * col


def second_kernel(kt_in, got, part_out, tot_out):
    last = scaled_round(kt_in, got)
    part_out[...] = jnp.sum(last, axis=0, keepdims=True)
    tot_out[...] = jnp.sum(got[:, :, last.shape[1] :], axis=0)


def third_kernel(kt_in, got, part_out, last_out):
    last = scaled_round(kt_in, got)
    last_out[...] = last
    part_out[...] = jnp.sum(last, axis=0, keepdims=True)


CHUNK = 256


def expos(rows, u):
    return jnp.exp(mul3(halves(rows), u, NN) / student_temp)


def student_kernel(
    index, turn, own, other, got, part, mine, given, f_own, f_other, w_out, u_out, n_out,
    s_scr, w_scr, tot_scr,
):
    _, n_blk, _, rows = tot_scr.shape
    all_rows, width = f_own.shape
    images = rows // CROPS
    n = all_rows // CHUNK
    raw = got[:, 1].reshape(width, got.shape[-1])
    norm = jnp.sqrt(jnp.sum(raw * raw, axis=0, keepdims=True) + norm_eps)
    unit = raw / norm
    u_out[...] = unit
    n_out[...] = norm
    u, v = halves(unit), halves(unit.T)
    for half, (pieces, f_out, message) in enumerate(((own, f_own, mine), (other, f_other, given))):
        src = s_scr.at[half]

        def put(j, place, few, piece):
            src[pl.ds(place + j * rows, few)] = piece

        assembled(turn, pieces, put, rows, 0)
        line = []
        for i in range(n):
            a, b = i * CHUNK, (i + 1) * CHUNK
            expo = expos(src[a:b], u)
            lanes = expo[:, :128]
            for k in range(1, expo.shape[1] // 128):
                lanes = lanes + expo[:, 128 * k : 128 * (k + 1)]
            line.append(jnp.sum(lanes.T, axis=0, keepdims=True))
            f_out[a:b] = mul3(halves(expo), v, NN)
        line = jnp.concatenate(line, axis=1)
        for j in range(n_blk):
            to = index[half * n_blk + j]
            tot_scr[half, to % n_blk] = line[:, j * rows : (j + 1) * rows]
            by_slot = src[j * rows : (j + 1) * rows].reshape(CROPS, images, width)
            local = jnp.sum(by_slot[GLOBAL_CROPS:], axis=0)
            w_scr[to, 0] = by_slot[1] + local
            w_scr[to, 1] = by_slot[0] + local
        message[...] = jnp.concatenate([part[...]] + [tot_scr[half, j] for j in range(n_blk)], axis=1)
    w_out[...] = w_scr[...].reshape(2 * n_blk * GLOBAL_CROPS * images, width).T


def grad_kernel(
    index, turn, own, other, tot_own, tot_other, unit, g_out, s_scr, tot_scr, *, coef
):
    _, all_rows, _ = s_scr.shape
    _, n_blk, _, rows = tot_scr.shape
    n = all_rows // CHUNK
    lane = lax.broadcasted_iota(jnp.int32, (1, rows), 1)
    count = jnp.where(lane < GLOBAL_CROPS * (rows // CROPS), GLOBAL_CROPS - 1.0, GLOBAL_CROPS * 1.0)
    u = halves(unit[...])
    g = None
    for half, (pieces, tot) in enumerate(((own, tot_own), (other, tot_other))):
        src = s_scr.at[half]

        def put(j, place, few, piece):
            src[pl.ds(place + j * rows, few)] = piece

        assembled(turn, pieces, put, rows, 0)
        for j in range(n_blk):
            tot_scr[half, j] = coef * count / tot[:, j * rows : (j + 1) * rows]
        scale = jnp.concatenate(
            [tot_scr[half, index[half * n_blk + j] % n_blk] for j in range(n_blk)], axis=1
        )
        for i in range(n):
            a, b = i * CHUNK, (i + 1) * CHUNK
            x = src[a:b]
            part = mul3(halves(x.T * scale[:, a:b]), halves(expos(x, u)), NN)
            g = part if g is None else g + part
    g_out[...] = g


def back_kernel(index, last, unit, own, other, scr):
    n_blk, rows, width = own.shape
    back = mul3(halves(last[...].T), halves(unit[...].T), NN)
    scr[...] = back.reshape(2 * n_blk, rows, width)
    for j in range(n_blk):
        own[j] = scr[index[j]]
        other[j] = scr[index[n_blk + j]]


def final_kernel(
    rate, got, last, weights, g_in, raw_in, unit_in, norm_in, next_out, row_out, *, coef
):
    width, cols = g_in.shape
    row = 1.0 / jnp.sum(got[...], axis=0)
    row_out[...] = row
    pulled = mul3(halves(weights[...] * (coef * row)), halves(last[...]), NT)
    g = g_in[...] - pulled
    unit = unit_in[...]
    along = jnp.sum(unit * g, axis=0, keepdims=True)
    proto_grad = (g - unit * along) / norm_in[...]
    square = jnp.mean(proto_grad * proto_grad, axis=0, keepdims=True)
    direction = proto_grad / jnp.sqrt(square + square_eps)
    raw = raw_in[:, 1].reshape(width, cols)
    new = raw - rate[0] * (direction + weight_decay * raw)
    next_out[...] = new.reshape(next_out.shape)


def other_core(v):
    return lax.ppermute(v, "c", ((0, 1), (1, 0)))


def spread_kernel(mine, theirs, out):
    out[...] = jnp.broadcast_to((mine[...] + theirs[...])[None], out.shape)


def everywhere(mine, given):
    theirs = other_core(given)
    n = lax.axis_size(CHIPS)
    (copies,) = call(spread_kernel, [VMEM, VMEM], [(VMEM, shape(n, *mine.shape))])(mine, theirs)
    return lax.all_to_all(copies, CHIPS, split_axis=0, concat_axis=0, tiled=True)


def shifted(v, axis, by):
    n = lax.axis_size(axis)
    return lax.ppermute(v, axis, [(i, (i + by) % n) for i in range(n)])


def mirrored(v):
    return lax.ppermute(v, ("zh", "zl"), [(i, 3 - i) for i in range(4)])


def gather_turns(v):
    v = jnp.stack([v, mirrored(v)])
    v = jnp.stack([v, shifted(v, "x", 3), shifted(v, "x", 2), shifted(v, "x", 1)])
    v = jnp.stack([v, shifted(v, "y", 3), shifted(v, "y", 2), shifted(v, "y", 1)])
    return v, other_core(v)


def scatter_chips(own, other):
    v = own + other_core(other)
    v = v[0] + shifted(v[1], "x", 1) + shifted(v[2], "x", 2) + shifted(v[3], "x", 3)
    return v


def scatter_rest(v):
    v = v[0] + mirrored(v[1])
    v = v + shifted(v, "zl", 1)
    v = v + lax.ppermute(v, "y", [(i, i ^ 1) for i in range(4)])
    return v + lax.ppermute(v, "y", [(i, 3 - i) for i in range(4)])


def body(student_feats, teacher_feats, student_proto, teacher_proto, crops, step):
    rate, teacher_temp, momentum = plan(step)
    n_dp = lax.axis_size(DP)
    own_rows, own_cols = student_proto.shape
    cols = own_cols // n_dp
    width = own_rows * n_dp
    crop_rows = student_feats.shape[0]
    teach_rows = teacher_feats.shape[0]
    images = teach_rows // GLOBAL_CROPS
    all_teach = n_dp * teach_rows
    pair_total = GLOBAL_CROPS * (GLOBAL_CROPS - 1) + (CROPS - GLOBAL_CROPS) * GLOBAL_CROPS
    coef = loss_scale / (pair_total * images * n_dp * student_temp)

    core, x, zh = lax.axis_index("c"), lax.axis_index("x"), lax.axis_index("zh")
    around = jnp.arange(n_dp, dtype=jnp.int32)
    index = (around // 8 ^ core) * 8 + (around // 2 + x) % 4 * 2 + (around % 2 ^ zh)

    turn = lax.axis_index("y")[None]
    n_turn = lax.axis_size("y")
    place = crops[:, 1] * images + crops[:, 0]
    both_rows = crop_rows + teach_rows
    (rows,) = call(
        rows_kernel,
        [SMEM, VMEM, VMEM, VMEM],
        [(VMEM, shape(both_rows // n_turn, width))],
        [room_for(crop_rows, width), room_for(teach_rows, width)],
        60 * 1024,
    )(turn, place[None, :], student_feats, teacher_feats)
    (pieces,) = call(
        pieces_kernel,
        [HBM, HBM],
        [(HBM, shape(n_dp, 2, own_rows, cols))],
        [room_for(own_rows, own_cols), room_for(own_rows, own_cols), DMA((2,)), DMA((n_dp, 2))],
        60 * 1024,
    )(teacher_proto, student_proto)
    got = lax.all_to_all(pieces, DP, split_axis=0, concat_axis=0, tiled=True)
    n_blk = n_dp // 2
    own, other = (
        v.reshape(n_turn, n_blk, both_rows // n_turn, width) for v in gather_turns(rows)
    )

    kt_shape = shape(cols, all_teach)
    kt, part = call(
        teacher_kernel,
        [SMEM, SMEM, SMEM, VMEM, VMEM, VMEM],
        [(VMEM, kt_shape), (VMEM, shape(1, all_teach))],
        [room_for(n_dp, teach_rows, width)],
    )(index, turn, teacher_temp[None], got, own, other)
    half = (n_blk * crop_rows, width)
    line = (1, n_blk * crop_rows)
    message = shape(1, all_teach + line[1])
    mine, given, f_own, f_other, weights, unit, norm = call(
        student_kernel,
        [SMEM, SMEM, VMEM, VMEM, VMEM, VMEM],
        [
            (VMEM, message),
            (VMEM, message),
            (VMEM, shape(*half)),
            (VMEM, shape(*half)),
            (VMEM, shape(width, all_teach)),
            (VMEM, shape(width, cols)),
            (VMEM, shape(1, cols)),
        ],
        [
            room_for(2, *half),
            room_for(n_dp, GLOBAL_CROPS, images, width),
            room_for(2, n_blk, 1, crop_rows),
        ],
    )(index, turn, own, other, got, part)
    sums = everywhere(mine, given)
    four = (4, 2, crop_rows, width)
    mine_s = scatter_chips(f_own.reshape(four), f_other.reshape(four))
    part, tot_own = call(
        second_kernel, [VMEM, VMEM], [(VMEM, shape(1, all_teach)), (VMEM, shape(*line))]
    )(kt, sums)
    tot_other = other_core(tot_own)
    sums = everywhere(part, part)
    part, last = call(
        third_kernel, [VMEM, VMEM], [(VMEM, shape(1, all_teach)), (VMEM, kt_shape)]
    )(kt, sums)
    sums = everywhere(part, part)

    b_own, b_other = call(
        back_kernel,
        [SMEM, VMEM, VMEM],
        [(VMEM, shape(n_blk, teach_rows, width))] * 2,
        [room_for(n_dp, teach_rows, width)],
    )(index, last, unit)
    four = (4, 2, teach_rows, width)
    mine_t = scatter_chips(b_own.reshape(four), b_other.reshape(four))
    mine = scatter_rest(jnp.concatenate([mine_s, mine_t], axis=1))
    mine_s, mine_t = mine[:crop_rows], mine[crop_rows:]

    (g,) = call(
        functools.partial(grad_kernel, coef=coef),
        [SMEM, SMEM, VMEM, VMEM, VMEM, VMEM, VMEM],
        [(VMEM, shape(width, cols))],
        [room_for(2, *half), room_for(2, n_blk, 1, crop_rows)],
    )(index, turn, own, other, tot_own, tot_other, unit)
    next_cols, row = call(
        functools.partial(final_kernel, coef=coef),
        [SMEM, VMEM, VMEM, VMEM, VMEM, VMEM, VMEM, VMEM],
        [(VMEM, shape(n_dp, own_rows, cols)), (VMEM, shape(1, all_teach))],
    )(rate[None], sums, last, weights, g, got, unit, norm)
    back = lax.all_to_all(next_cols, DP, split_axis=0, concat_axis=0, tiled=True)
    student_next = back.transpose(1, 0, 2).reshape(own_rows, own_cols)
    teacher_next = momentum * teacher_proto + (1.0 - momentum) * student_next

    my_block = x * 2 + zh
    my_total = lax.dynamic_index_in_dim(tot_own.reshape(n_blk, crop_rows), my_block, 0, keepdims=False)
    my_row = lax.dynamic_index_in_dim(row.reshape(n_dp, teach_rows), core * 8 + my_block, 0, keepdims=False)
    slots = jnp.arange(crop_rows) // images
    count = jnp.where(slots < GLOBAL_CROPS, GLOBAL_CROPS - 1.0, GLOBAL_CROPS * 1.0)
    scale = coef * count / my_total
    part_t = (coef * my_row[:, None] * mine_t).reshape(GLOBAL_CROPS, images, width)
    both_t = part_t[0] + part_t[1]
    target = jnp.concatenate(
        [part_t[1][None], part_t[0][None], jnp.broadcast_to(both_t, (CROPS - GLOBAL_CROPS, *both_t.shape))]
    ).reshape(crop_rows, width)
    feature_sorted = mine_s * scale[:, None] - target
    q_iota = lax.broadcasted_iota(jnp.int32, (crop_rows, crop_rows), 0)
    sort = (q_iota == place[None, :]).astype(f32)
    feature_unit = dot(sort, feature_sorted, ((0,), (0,)), highest)
    s_norm = jnp.sqrt(jnp.sum(student_feats * student_feats, axis=1, keepdims=True) + norm_eps)
    s_unit = student_feats / s_norm
    feature_grad = (
        feature_unit - s_unit * jnp.sum(s_unit * feature_unit, axis=1, keepdims=True)
    ) / s_norm
    return (student_next, teacher_next, feature_grad)


def solution(mesh):
    n_x, n_zh, n_c, n_y, n_zl = 4, 2, 2, 4, 2
    fine = Mesh(mesh.devices.reshape(n_x, n_zh, n_c, n_y, n_zl), AXES)
    in_specs = (P(DP, None), P(DP, None), P(DP, PROTO), P(DP, PROTO), P(DP, None), P())
    out_specs = (P(DP, PROTO), P(DP, PROTO), P(DP, None))
    return jax.shard_map(body, mesh=fine, in_specs=in_specs, out_specs=out_specs, check_vma=False)
```

time: 283 us -> 195 us (0.69); the launches traced: 277 us -> 193 us
  waiting for transfers between devices: 146 us -> 65.1 us
  blocking collectives: 0 us -> 31.6 us
  starting transfers between devices: 76.3 us -> 50.3 us
  Pallas kernels: 0 us -> 25.3 us
  matrix products: 16.8 us -> 0.49 us
  local copies, waits for them, and re-layouts: 19.6 us -> 7.22 us
  other arithmetic: 16.5 us -> 11.7 us
    all_to_all x10 -> x3, waiting for transfers between devices: 138 us -> 15.1 us  [the longest x1 15.1 us: body(): got = lax.all_to_all(pieces, DP, split_axis=0, concat_axis=0, tiled=True)]
    all_to_all x10 -> x3, starting transfers between devices: 58.2 us -> 14.5 us  [the longest x1 6.27 us: body(): lax.all_to_all(next_cols, DP, split_axis=0, concat_axis=0, tiled=True)]
    all_to_all x0 -> x2, blocking collectives: none -> 31.6 us  [everywhere(): lax.all_to_all(copies, CHIPS, split_axis=0, concat_axis=0, tiled=True)]
    ppermute x9 -> x13, waiting for transfers between devices: 6.16 us -> 34.1 us  [shifted(): return lax.ppermute(v, axis, [(i, (i + by) % n) for i in range(n)])]
    pallas_call x0 -> x12, Pallas kernels: none -> 25.3 us  [the longest x1 7.64 us: body(): call(functools.partial(grad_kernel, coef=coef), [SMEM, SMEM, VMEM, VMEM,...]
    dot_general x8 -> x1, matrix products: 16.8 us -> 0.49 us  [dot(): lax.dot_general(a, b, (dims, ((), ())), precision=precision, preferred_el...]
    ppermute x0 -> x4, waiting for transfers between devices: none -> 9.82 us  [the longest x1 4.25 us: scatter_rest(): return v + lax.ppermute(v, 'y', [(i, 3 - i) for i in range(4)])]
    reduce_sum x18 -> x1, other arithmetic: 7.77 us -> 0.11 us  [body(): jnp.sum(student_feats * student_feats, axis=1, keepdims=True) + norm_eps]
  transfers between devices with their start and end apart: 23 -> 27, of which waited for: 17 -> 18; matrix products, arithmetic and copies ran while one was open for 8% -> 5% of each run, Pallas kernels for 0% -> 8%
where the time goes in v2:
time: 195 us; the launch traced here: 193 us
  waiting for transfers between devices  65.1 us (33%)
  starting transfers between devices  50.3 us (26%)
  blocking collectives  31.6 us (16%)
  Pallas kernels  25.3 us (13%)
  other arithmetic  11.7 us (6%)
  local copies, waits for them, and re-layouts  7.22 us (4%)
    ppermute x13, waiting for transfers between devices, shifted(): return lax.ppermute(v, axis, [(i, (i + by) % n) for i in range(n)])  34.1 us
    all_to_all x2, blocking collectives, everywhere(): lax.all_to_all(copies, CHIPS, split_axis=0, concat_axis=0, tiled=True)  31.6 us
    ppermute x13, starting transfers between devices, shifted(): return lax.ppermute(v, axis, [(i, (i + by) % n) for i in range(n)])  17.4 us
    all_to_all x1, waiting for transfers between devices, body(): got = lax.all_to_all(pieces, DP, split_axis=0, concat_axis=0, tiled=True)  15.1 us
    ppermute x7, starting transfers between devices, other_core(): return lax.ppermute(v, 'c', ((0, 1), (1, 0)))  11.7 us
    pallas_call x1, Pallas kernels, body(): call(functools.partial(grad_kernel, coef=coef), [SMEM, SMEM, VMEM, VMEM,...  7.64 us
    pallas_call x1, Pallas kernels, body(): call(student_kernel, [SMEM, SMEM, VMEM, VMEM, VMEM, VMEM], [(VMEM, messag...  6.37 us
    all_to_all x1, starting transfers between devices, body(): lax.all_to_all(next_cols, DP, split_axis=0, concat_axis=0, tiled=True)  6.27 us
  transfers between devices with their start and end apart: 27, of which 18 were waited for; matrix products, arithmetic and copies ran while one was open for 5% of the time, Pallas kernels for 8%

profile of v2, /device:TPU:1, one launch (start us, length us, event | category | flops | bytes accessed | tf_op | source)
XLA Modules:
  0.0 193.4 jit_solution(14062186843848181614)
XLA Ops:
  2.0 1.9 shard_map.86
  3.8 4.6 %collective-permute-start = (f32[48,256]{1,0:T(8,128)}, f32[48,256]{1,0:T(8,128)S(1)}, u32[]{:S(2)}, u32[]{:S(2)}) collective-permute-start(f32[48,256]{1,0:T(8,128)} %shard_map.86), channel_id=1, source_target_pairs={{0,17},{1,16},{16,1},{17,0},{2,19},{3,18},{18,3},{19,2},{4,21},{5,... | collective-permute-start | bytes 147464 | tf_op jit(solution)/shard_map/ppermute | solution.py:312
  8.4 1.7 collective-permute-done
  10.9 2.8 %collective-permute-start.2 = (f32[2,48,256]{2,1,0:T(8,128)S(1)}, f32[2,48,256]{2,1,0:T(8,128)S(1)}, u32[]{:S(2)}, u32[]{:S(2)}) collective-permute-start(f32[2,48,256]{2,1,0:T(8,128)S(1)} %get-tuple-element.46), channel_id=1, source_target_pairs={{0,64},{32,96},{64,0},{96,32},{1,65},{33,97},{65,1},{97,33},{2,66}... | collective-permute-start | bytes 294920 | tf_op jit(solution)/shard_map/ppermute | solution.py:308
  16.0 1.7 collective-permute-done.1
  17.7 2.0 %collective-permute-done.3 = f32[2,48,256]{2,1,0:T(8,128)S(1)} collective-permute-done((f32[2,48,256]{2,1,0:T(8,128)S(1)}, f32[2,48,256]{2,1,0:T(8,128)S(1)}, u32[]{:S(2)}, u32[]{:S(2)}) %collective-permute-start.3) | collective-permute-done | bytes 98336 | tf_op jit(solution)/shard_map/ppermute | solution.py:308
  21.1 2.6 %collective-permute-start.5 = (f32[4,2,48,256]{3,2,1,0:T(8,128)S(1)}, f32[4,2,48,256]{3,2,1,0:T(8,128)S(1)}, u32[]{:S(2)}, u32[]{:S(2)}) collective-permute-start(f32[4,2,48,256]{3,2,1,0:T(8,128)S(1)} %get-tuple-element.41), channel_id=1, source_target_pairs={{0,4},{2,6},{4,0},{6,2},{1,5},{3,7},{5,1},{7,3},{8,12},{10,14},{12... | collective-permute-start | bytes 1179656 | tf_op jit(solution)/shard_map/ppermute | solution.py:308
  24.8 4.2 %collective-permute-done.6 = f32[4,2,48,256]{3,2,1,0:T(8,128)S(1)} collective-permute-done((f32[4,2,48,256]{3,2,1,0:T(8,128)S(1)}, f32[4,2,48,256]{3,2,1,0:T(8,128)S(1)}, u32[]{:S(2)}, u32[]{:S(2)}) %collective-permute-start.6) | collective-permute-done | bytes 393248 | tf_op jit(solution)/shard_map/ppermute | solution.py:308
  29.0 9.5 %collective-permute-done.5 = f32[4,2,48,256]{3,2,1,0:T(8,128)S(1)} collective-permute-done((f32[4,2,48,256]{3,2,1,0:T(8,128)S(1)}, f32[4,2,48,256]{3,2,1,0:T(8,128)S(1)}, u32[]{:S(2)}, u32[]{:S(2)}) %collective-permute-start.5) | collective-permute-done | bytes 393248 | tf_op jit(solution)/shard_map/ppermute | solution.py:308
  41.2 2.3 %collective-permute-start.7 = (f32[4,4,2,48,256]{4,3,2,1,0:T(8,128)}, f32[4,4,2,48,256]{4,3,2,1,0:T(8,128)}, u32[]{:S(2)}, u32[]{:S(2)}) collective-permute-start(f32[4,4,2,48,256]{4,3,2,1,0:T(8,128)} %pad_maximum_fusion.1), channel_id=1, source_target_pairs={{0,8},{8,0},{1,9},{9,1},{2,10},{10,2},{3,11},{11,3},{4,12},{12,4},... | collective-permute-start | bytes 4718600 | tf_op jit(solution)/shard_map/ppermute | solution.py:292
  43.6 2.3 %shard_map.85 = f32[16,2,16,512]{3,2,1,0:T(8,128)} custom-call(f32[16,8192]{1,0:T(8,128)} %tp.1, f32[16,8192]{1,0:T(8,128)} %sp.1), custom_call_target="tpu_custom_call" | custom-call | tf_op jit(solution)/shard_map/pallas_call | solution.py:363
  45.9 3.6 %all-to-all-start = ((f32[16,2,16,512]{3,2,1,0:T(8,128)}), f32[16,2,16,512]{3,2,1,0:T(8,128)S(1)}, u32[]{:S(2)}, u32[]{:S(2)}) async-start(f32[16,2,16,512]{3,2,1,0:T(8,128)} %shard_map.85), calls=%async_computation | async-start | bytes 2097152 | tf_op jit(solution)/shard_map/all_to_all | solution.py:370
  51.4 15.1 %all-to-all-done.got.raw_in = f32[16,2,16,512]{3,2,1,0:T(8,128)S(1)} async-done(((f32[16,2,16,512]{3,2,1,0:T(8,128)}), f32[16,2,16,512]{3,2,1,0:T(8,128)S(1)}, u32[]{:S(2)}, u32[]{:S(2)}) %all-to-all-start) | async-done | bytes 1048608 | tf_op jit(solution)/shard_map/all_to_all | solution.py:370
  66.4 2.3 %shard_map.87 = (f32[512,512]{1,0:T(8,128)S(1)}, f32[1,512]{1,0:T(1,128)S(1)}) custom-call(s32[16]{0:T(128)S(1)} %fusion.18.index, s32[1]{0:T(128)} %bitcast.turn, f32[1]{0:T(128)S(6)} %add_shard_map.9.temp, f32[16,2,16,512]{3,2,1,0:T(8,128)S(1)} %all-to-all-done.got.raw_in, f32[4,8,48,256]{3,2,1,0:T(8,128)S(1)} %pad_maximum_fusion.own, ...), custom_call_target="tpu_custom_call" | custom-call | tf_op jit(solution)/shard_map/pallas_call | solution.py:377
  68.7 6.4 %shard_map.88 = (f32[1,1792]{1,0:T(1,128)S(1)}, f32[1,1792]{1,0:T(1,128)S(1)}, f32[1280,256]{1,0:T(8,128)S(1)}, f32[1280,256]{1,0:T(8,128)S(1)}, f32[256,512]{1,...) custom-call(s32[16]{0:T(128)S(1)} %fusion.18.index, s32[1]{0:T(128)} %bitcast.turn, ...), custom_call_target="tpu_custom_call" | custom-call | tf_op jit(solution)/shard_map/pallas_call | solution.py:386
  76.3 2.6 %collective-permute-done.8.theirs = f32[1,1792]{1,0:T(1,128)S(1)} collective-permute-done((f32[1,1792]{1,0:T(1,128)S(1)}, f32[1,1792]{1,0:T(1,128)S(1)}, u32[]{:S(2)}, u32[]{:S(2)}) %collective-permute-start.8) | collective-permute-done | bytes 7200 | tf_op jit(solution)/shard_map/ppermute | solution.py:292
  78.9 18.6 %all_to_all.25.got = f32[64,1,1792]{2,1,0:T(1,128)S(1)} all-to-all(f32[64,1,1792]{2,1,0:T(1,128)S(1)} %shard_map.89), channel_id=1, replica_groups=mesh['x'=4,'zh'=2,'c'=2,'y'=4,'zl'=2] {'x','zh','y','zl'}, dimensions={0} | all-to-all | bytes 917504 | tf_op jit(solution)/shard_map/all_to_all | solution.py:303
  98.1 1.7 collective-permute-start.9
  100.6 12.9 %all_to_all.26.got = f32[64,1,512]{2,1,0:T(1,128)S(1)} all-to-all(f32[64,1,512]{2,1,0:T(1,128)S(1)} %shard_map.91), channel_id=1, replica_groups=mesh['x'=4,'zh'=2,'c'=2,'y'=4,'zl'=2] {'x','zh','y','zl'}, dimensions={0} | all-to-all | bytes 262144 | tf_op jit(solution)/shard_map/all_to_all | solution.py:303
  113.8 1.5 shard_map.96
  115.4 1.8 collective-permute-start.16
  120.9 2.5 %collective-permute-start.15 = (f32[2,160,256]{2,1,0:T(8,128)}, f32[2,160,256]{2,1,0:T(8,128)}, u32[]{:S(2)}, u32[]{:S(2)}) collective-permute-start(f32[2,160,256]{2,1,0:T(8,128)} %get-tuple-element.38), channel_id=1, source_target_pairs={{0,96},{32,0},{64,32},{96,64},{1,97},{33,1},{65,33},{97,65},{2,98}... | collective-permute-start | bytes 983048 | tf_op jit(solution)/shard_map/ppermute | solution.py:308
  127.1 2.1 %collective-permute-start.18 = (f32[2,32,256]{2,1,0:T(8,128)}, f32[2,32,256]{2,1,0:T(8,128)}, u32[]{:S(2)}, u32[]{:S(2)}) collective-permute-start(f32[2,32,256]{2,1,0:T(8,128)} %get-tuple-element.44), channel_id=1, source_target_pairs={{0,64},{32,96},{64,0},{96,32},{1,65},{33,97},{65,1},{97,33},{2,66}... | collective-permute-start | bytes 196616 | tf_op jit(solution)/shard_map/ppermute | solution.py:308
  129.9 4.6 %all-to-all-start.3 = ((f32[64,1,512]{2,1,0:T(1,128)}), f32[64,1,512]{2,1,0:T(1,128)S(1)}, u32[]{:S(2)}, u32[]{:S(2)}) async-start(f32[64,1,512]{2,1,0:T(1,128)} %shard_map.93), calls=%async_computation.3 | async-start | bytes 262144 | tf_op jit(solution)/shard_map/all_to_all | solution.py:303
  134.5 4.5 %collective-permute-done.19 = f32[2,32,256]{2,1,0:T(8,128)S(1)} collective-permute-done((f32[2,32,256]{2,1,0:T(8,128)}, f32[2,32,256]{2,1,0:T(8,128)S(1)}, u32[]{:S(2)}, u32[]{:S(2)}) %collective-permute-start.19) | collective-permute-done | bytes 65568 | tf_op jit(solution)/shard_map/ppermute | solution.py:308
  143.8 3.4 %collective-permute-start.11 = (f32[1,1280]{1,0:T(1,128)S(1)}, f32[1,1280]{1,0:T(1,128)S(1)}, u32[]{:S(2)}, u32[]{:S(2)}) collective-permute-start(f32[1,1280]{1,0:T(1,128)S(1)} %get-tuple-element.28.tot_own), channel_id=1, source_target_pairs={{0,8},{8,0},{1,9},{9,1},{2,10},{10,2},{3,11},{11,3},{4,12},{12,4},... | collective-permute-start | bytes 15368 | tf_op jit(solution)/shard_map/ppermute | solution.py:292
  148.1 7.6 %shard_map.94.g_in = f32[256,512]{1,0:T(8,128)S(1)} custom-call(s32[16]{0:T(128)S(1)} %fusion.18.index, s32[1]{0:T(128)} %bitcast.turn, f32[4,8,48,256]{3,2,1,0:T(8,128)S(1)} %pad_maximum_fusion.own, f32[4,8,48,256]{3,2,1,0:T(8,128)} %bitcast.16.other, f32[1,1280]{1,0:T(1,128)S(1)} %get-tuple-element.28.tot_own, ...), custom_call_target="tpu_custom_call" | custom-call | tf_op jit(solution)/shard_map/pallas_call | solution.py:428
  159.8 1.8 shard_map.95
  161.7 6.3 %all-to-all-start.4 = ((f32[16,16,512]{2,1,0:T(8,128)}), f32[16,16,512]{2,1,0:T(8,128)S(1)}, u32[]{:S(2)}, u32[]{:S(2)}) async-start(f32[16,16,512]{2,1,0:T(8,128)} %get-tuple-element.31), calls=%async_computation.4 | async-start | bytes 1048576 | tf_op jit(solution)/shard_map/all_to_all | solution.py:439
  170.6 9.5 %collective-permute-done.21 = f32[192,256]{1,0:T(8,128)S(1)} collective-permute-done((f32[192,256]{1,0:T(8,128)S(1)}, f32[192,256]{1,0:T(8,128)S(1)}, u32[]{:S(2)}, u32[]{:S(2)}) %collective-permute-start.21) | collective-permute-done | bytes 196640 | tf_op jit(solution)/shard_map/ppermute | solution.py:308
  182.0 3.9 %collective-permute-done.22 = f32[192,256]{1,0:T(8,128)S(1)} collective-permute-done((f32[192,256]{1,0:T(8,128)S(1)}, f32[192,256]{1,0:T(8,128)S(1)}, u32[]{:S(2)}, u32[]{:S(2)}) %collective-permute-start.22) | collective-permute-done | bytes 196640 | tf_op jit(solution)/shard_map/ppermute | solution.py:331
  187.8 4.3 %collective-permute-done.23 = f32[192,256]{1,0:T(8,128)S(1)} collective-permute-done((f32[192,256]{1,0:T(8,128)S(1)}, f32[192,256]{1,0:T(8,128)S(1)}, u32[]{:S(2)}, u32[]{:S(2)}) %collective-permute-start.23) | collective-permute-done | bytes 196640 | tf_op jit(solution)/shard_map/ppermute | solution.py:332
  (106 shorter events, 39.1 us)
Async XLA Ops:
  3.8 6.3 %collective-permute-start = (f32[48,256]{1,0:T(8,128)}, f32[48,256]{1,0:T(8,128)S(1)}, u32[]{:S(2)}, u32[]{:S(2)}) collective-permute-start(f32[48,256]{1,0:T(8,128)} %shard_map.86), channel_id=1, source_target_pairs={{0,17},{1,16},{16,1},{17,0},{2,19},{3,18},{18,3},{19,2},{4,21},{5,... | collective-permute-start | bytes 147464 | tf_op jit(solution)/shard_map/ppermute | solution.py:312
  10.9 5.1 %collective-permute-start.2 = (f32[2,48,256]{2,1,0:T(8,128)S(1)}, f32[2,48,256]{2,1,0:T(8,128)S(1)}, u32[]{:S(2)}, u32[]{:S(2)}) collective-permute-start(f32[2,48,256]{2,1,0:T(8,128)S(1)} %get-tuple-element.46), channel_id=1, source_target_pairs={{0,64},{32,96},{64,0},{96,32},{1,65},{33,97},{65,1},{97,33},{2,66}... | collective-permute-start | bytes 294920 | tf_op jit(solution)/shard_map/ppermute | solution.py:308
  13.8 4.0 %collective-permute-start.1 = (f32[2,48,256]{2,1,0:T(8,128)S(1)}, f32[2,48,256]{2,1,0:T(8,128)S(1)}, u32[]{:S(2)}, u32[]{:S(2)}) collective-permute-start(f32[2,48,256]{2,1,0:T(8,128)S(1)} %get-tuple-element.46), channel_id=1, source_target_pairs={{0,96},{32,0},{64,32},{96,64},{1,97},{33,1},{65,33},{97,65},{2,98}... | collective-permute-start | bytes 294920 | tf_op jit(solution)/shard_map/ppermute | solution.py:308
  14.6 5.1 %collective-permute-start.3 = (f32[2,48,256]{2,1,0:T(8,128)S(1)}, f32[2,48,256]{2,1,0:T(8,128)S(1)}, u32[]{:S(2)}, u32[]{:S(2)}) collective-permute-start(f32[2,48,256]{2,1,0:T(8,128)S(1)} %get-tuple-element.46), channel_id=1, source_target_pairs={{0,32},{32,64},{64,96},{96,0},{1,33},{33,65},{65,97},{97,1},{2,34}... | collective-permute-start | bytes 294920 | tf_op jit(solution)/shard_map/ppermute | solution.py:308
  19.8 21.5 %copy-start.11 = (f32[4,2,48,256]{3,2,1,0:T(8,128)}, f32[4,2,48,256]{3,2,1,0:T(8,128)S(1)}, u32[]{:S(2)}) copy-start(f32[4,2,48,256]{3,2,1,0:T(8,128)S(1)} %get-tuple-element.41) | copy-start | bytes 1179652
  19.8 9.2 %collective-permute-start.6 = (f32[4,2,48,256]{3,2,1,0:T(8,128)S(1)}, f32[4,2,48,256]{3,2,1,0:T(8,128)S(1)}, u32[]{:S(2)}, u32[]{:S(2)}) collective-permute-start(f32[4,2,48,256]{3,2,1,0:T(8,128)S(1)} %get-tuple-element.41), channel_id=1, source_target_pairs={{0,2},{2,4},{4,6},{6,0},{1,3},{3,5},{5,7},{7,1},{8,10},{10,12},{12... | collective-permute-start | bytes 1179656 | tf_op jit(solution)/shard_map/ppermute | solution.py:308
  21.1 17.4 %collective-permute-start.5 = (f32[4,2,48,256]{3,2,1,0:T(8,128)S(1)}, f32[4,2,48,256]{3,2,1,0:T(8,128)S(1)}, u32[]{:S(2)}, u32[]{:S(2)}) collective-permute-start(f32[4,2,48,256]{3,2,1,0:T(8,128)S(1)} %get-tuple-element.41), channel_id=1, source_target_pairs={{0,4},{2,6},{4,0},{6,2},{1,5},{3,7},{5,1},{7,3},{8,12},{10,14},{12... | collective-permute-start | bytes 1179656 | tf_op jit(solution)/shard_map/ppermute | solution.py:308
  23.8 16.2 %collective-permute-start.4 = (f32[4,2,48,256]{3,2,1,0:T(8,128)S(1)}, f32[4,2,48,256]{3,2,1,0:T(8,128)S(1)}, u32[]{:S(2)}, u32[]{:S(2)}) collective-permute-start(f32[4,2,48,256]{3,2,1,0:T(8,128)S(1)} %get-tuple-element.41), channel_id=1, source_target_pairs={{0,6},{2,0},{4,2},{6,4},{1,7},{3,1},{5,3},{7,5},{8,14},{10,8},{12,... | collective-permute-start | bytes 1179656 | tf_op jit(solution)/shard_map/ppermute | solution.py:308
  41.2 25.2 %collective-permute-start.7 = (f32[4,4,2,48,256]{4,3,2,1,0:T(8,128)}, f32[4,4,2,48,256]{4,3,2,1,0:T(8,128)}, u32[]{:S(2)}, u32[]{:S(2)}) collective-permute-start(f32[4,4,2,48,256]{4,3,2,1,0:T(8,128)} %pad_maximum_fusion.1), channel_id=1, source_target_pairs={{0,8},{8,0},{1,9},{9,1},{2,10},{10,2},{3,11},{11,3},{4,12},{12,4},... | collective-permute-start | bytes 4718600 | tf_op jit(solution)/shard_map/ppermute | solution.py:292
  45.9 20.5 %all-to-all-start = ((f32[16,2,16,512]{3,2,1,0:T(8,128)}), f32[16,2,16,512]{3,2,1,0:T(8,128)S(1)}, u32[]{:S(2)}, u32[]{:S(2)}) async-start(f32[16,2,16,512]{3,2,1,0:T(8,128)} %shard_map.85), calls=%async_computation | async-start | bytes 2097152 | tf_op jit(solution)/shard_map/all_to_all | solution.py:370
  75.1 38.5 %copy-start.4 = (f32[256,512]{1,0:T(8,128)}, f32[256,512]{1,0:T(8,128)S(1)}, u32[]{:S(2)}) copy-start(f32[256,512]{1,0:T(8,128)S(1)} %get-tuple-element.27.weights) | copy-start | bytes 1572868
  75.1 44.4 %collective-permute-start.12 = (f32[4,2,160,256]{3,2,1,0:T(8,128)S(1)}, f32[4,2,160,256]{3,2,1,0:T(8,128)S(1)}, u32[]{:S(2)}, u32[]{:S(2)}) collective-permute-start(f32[4,2,160,256]{3,2,1,0:T(8,128)S(1)} %bitcast.73), channel_id=1, source_target_pairs={{0,8},{8,0},{1,9},{9,1},{2,10},{10,2},{3,11},{11,3},{4,12},{12,4},... | collective-permute-start | bytes 3932168 | tf_op jit(solution)/shard_map/ppermute | solution.py:292
  76.2 2.7 %collective-permute-start.8 = (f32[1,1792]{1,0:T(1,128)S(1)}, f32[1,1792]{1,0:T(1,128)S(1)}, u32[]{:S(2)}, u32[]{:S(2)}) collective-permute-start(f32[1,1792]{1,0:T(1,128)S(1)} %get-tuple-element.23), channel_id=1, source_target_pairs={{0,8},{8,0},{1,9},{9,1},{2,10},{10,2},{3,11},{11,3},{4,12},{12,4},... | collective-permute-start | bytes 21512 | tf_op jit(solution)/shard_map/ppermute | solution.py:292
  98.1 2.5 %collective-permute-start.9 = (f32[1,512]{1,0:T(1,128)S(1)}, f32[1,512]{1,0:T(1,128)S(1)}, u32[]{:S(2)}, u32[]{:S(2)}) collective-permute-start(f32[1,512]{1,0:T(1,128)S(1)} %get-tuple-element.24.mine), channel_id=1, source_target_pairs={{0,8},{8,0},{1,9},{9,1},{2,10},{10,2},{3,11},{11,3},{4,12},{12,4},... | collective-permute-start | bytes 6152 | tf_op jit(solution)/shard_map/ppermute | solution.py:292
  115.4 3.0 %collective-permute-start.16 = (f32[4,2,32,256]{3,2,1,0:T(8,128)S(1)}, f32[4,2,32,256]{3,2,1,0:T(8,128)S(1)}, u32[]{:S(2)}, u32[]{:S(2)}) collective-permute-start(f32[4,2,32,256]{3,2,1,0:T(8,128)S(1)} %bitcast.74), channel_id=1, source_target_pairs={{0,8},{8,0},{1,9},{9,1},{2,10},{10,2},{3,11},{11,3},{4,12},{12,4},... | collective-permute-start | bytes 786440 | tf_op jit(solution)/shard_map/ppermute | solution.py:292
  119.1 8.0 %collective-permute-start.17 = (f32[2,32,256]{2,1,0:T(8,128)S(1)}, f32[2,32,256]{2,1,0:T(8,128)S(1)}, u32[]{:S(2)}, u32[]{:S(2)}) collective-permute-start(f32[2,32,256]{2,1,0:T(8,128)S(1)} %get-tuple-element.42), channel_id=1, source_target_pairs={{0,32},{32,64},{64,96},{96,0},{1,33},{33,65},{65,97},{97,1},{2,34}... | collective-permute-start | bytes 196616 | tf_op jit(solution)/shard_map/ppermute | solution.py:308
  120.8 23.1 %copy-start.16 = (s32[160,2]{0,1:T(2,128)S(1)}, s32[160,2]{0,1:T(2,128)}, u32[]{:S(2)}) copy-start(s32[160,2]{0,1:T(2,128)} %param.10) | copy-start | bytes 3844
  120.8 26.5 %copy-start.12 = (f32[160,256]{1,0:T(8,128)S(1)}, f32[160,256]{1,0:T(8,128)}, u32[]{:S(2)}) copy-start(f32[160,256]{1,0:T(8,128)} %sf.1) | copy-start | bytes 491524
  120.8 20.3 %collective-permute-start.13 = (f32[2,160,256]{2,1,0:T(8,128)}, f32[2,160,256]{2,1,0:T(8,128)}, u32[]{:S(2)}, u32[]{:S(2)}) collective-permute-start(f32[2,160,256]{2,1,0:T(8,128)} %get-tuple-element.37), channel_id=1, source_target_pairs={{0,32},{32,64},{64,96},{96,0},{1,33},{33,65},{65,97},{97,1},{2,34}... | collective-permute-start | bytes 983048 | tf_op jit(solution)/shard_map/ppermute | solution.py:308
  120.9 20.2 %collective-permute-start.15 = (f32[2,160,256]{2,1,0:T(8,128)}, f32[2,160,256]{2,1,0:T(8,128)}, u32[]{:S(2)}, u32[]{:S(2)}) collective-permute-start(f32[2,160,256]{2,1,0:T(8,128)} %get-tuple-element.38), channel_id=1, source_target_pairs={{0,96},{32,0},{64,32},{96,64},{1,97},{33,1},{65,33},{97,65},{2,98}... | collective-permute-start | bytes 983048 | tf_op jit(solution)/shard_map/ppermute | solution.py:308
  123.4 17.7 %collective-permute-start.14 = (f32[2,160,256]{2,1,0:T(8,128)}, f32[2,160,256]{2,1,0:T(8,128)}, u32[]{:S(2)}, u32[]{:S(2)}) collective-permute-start(f32[2,160,256]{2,1,0:T(8,128)} %get-tuple-element.39), channel_id=1, source_target_pairs={{0,64},{32,96},{64,0},{96,32},{1,65},{33,97},{65,1},{97,33},{2,66}... | collective-permute-start | bytes 983048 | tf_op jit(solution)/shard_map/ppermute | solution.py:308
  124.2 2.0 %collective-permute-start.10 = (f32[1,512]{1,0:T(1,128)S(1)}, f32[1,512]{1,0:T(1,128)S(1)}, u32[]{:S(2)}, u32[]{:S(2)}) collective-permute-start(f32[1,512]{1,0:T(1,128)S(1)} %get-tuple-element.25.mine), channel_id=1, source_target_pairs={{0,8},{8,0},{1,9},{9,1},{2,10},{10,2},{3,11},{11,3},{4,12},{12,4},... | collective-permute-start | bytes 6152 | tf_op jit(solution)/shard_map/ppermute | solution.py:292
  126.3 12.7 %collective-permute-start.19 = (f32[2,32,256]{2,1,0:T(8,128)}, f32[2,32,256]{2,1,0:T(8,128)S(1)}, u32[]{:S(2)}, u32[]{:S(2)}) collective-permute-start(f32[2,32,256]{2,1,0:T(8,128)} %get-tuple-element.43), channel_id=1, source_target_pairs={{0,96},{32,0},{64,32},{96,64},{1,97},{33,1},{65,33},{97,65},{2,98}... | collective-permute-start | bytes 196616 | tf_op jit(solution)/shard_map/ppermute | solution.py:308
  127.1 13.0 %collective-permute-start.18 = (f32[2,32,256]{2,1,0:T(8,128)}, f32[2,32,256]{2,1,0:T(8,128)}, u32[]{:S(2)}, u32[]{:S(2)}) collective-permute-start(f32[2,32,256]{2,1,0:T(8,128)} %get-tuple-element.44), channel_id=1, source_target_pairs={{0,64},{32,96},{64,0},{96,32},{1,65},{33,97},{65,1},{97,33},{2,66}... | collective-permute-start | bytes 196616 | tf_op jit(solution)/shard_map/ppermute | solution.py:308
  129.9 26.6 %all-to-all-start.3 = ((f32[64,1,512]{2,1,0:T(1,128)}), f32[64,1,512]{2,1,0:T(1,128)S(1)}, u32[]{:S(2)}, u32[]{:S(2)}) async-start(f32[64,1,512]{2,1,0:T(1,128)} %shard_map.93), calls=%async_computation.3 | async-start | bytes 262144 | tf_op jit(solution)/shard_map/all_to_all | solution.py:303
  143.2 24.7 %collective-permute-start.20 = (f32[192,256]{1,0:T(8,128)}, f32[192,256]{1,0:T(8,128)}, u32[]{:S(2)}, u32[]{:S(2)}) collective-permute-start(f32[192,256]{1,0:T(8,128)} %fusion.6), channel_id=1, source_target_pairs={{0,17},{1,16},{16,1},{17,0},{2,19},{3,18},{18,3},{19,2},{4,21},{5,... | collective-permute-start | bytes 589832 | tf_op jit(solution)/shard_map/ppermute | solution.py:312
  143.8 4.2 %collective-permute-start.11 = (f32[1,1280]{1,0:T(1,128)S(1)}, f32[1,1280]{1,0:T(1,128)S(1)}, u32[]{:S(2)}, u32[]{:S(2)}) collective-permute-start(f32[1,1280]{1,0:T(1,128)S(1)} %get-tuple-element.28.tot_own), channel_id=1, source_target_pairs={{0,8},{8,0},{1,9},{9,1},{2,10},{10,2},{3,11},{11,3},{4,12},{12,4},... | collective-permute-start | bytes 15368 | tf_op jit(solution)/shard_map/ppermute | solution.py:292
  161.7 20.2 %all-to-all-start.4 = ((f32[16,16,512]{2,1,0:T(8,128)}), f32[16,16,512]{2,1,0:T(8,128)S(1)}, u32[]{:S(2)}, u32[]{:S(2)}) async-start(f32[16,16,512]{2,1,0:T(8,128)} %get-tuple-element.31), calls=%async_computation.4 | async-start | bytes 1048576 | tf_op jit(solution)/shard_map/all_to_all | solution.py:439
  167.9 18.9 %copy-start.9 = (f32[16,8192]{1,0:T(8,128)S(1)}, f32[16,8192]{1,0:T(8,128)}, u32[]{:S(2)}) copy-start(f32[16,8192]{1,0:T(8,128)} %tp.1) | copy-start | bytes 1572868
  169.1 11.0 %collective-permute-start.21 = (f32[192,256]{1,0:T(8,128)S(1)}, f32[192,256]{1,0:T(8,128)S(1)}, u32[]{:S(2)}, u32[]{:S(2)}) collective-permute-start(f32[192,256]{1,0:T(8,128)S(1)} %fusion.5), channel_id=1, source_target_pairs={{0,1},{1,0},{2,3},{3,2},{4,5},{5,4},{6,7},{7,6},{8,9},{9,8},{10,11... | collective-permute-start | bytes 589832 | tf_op jit(solution)/shard_map/ppermute | solution.py:308
  180.1 5.8 %collective-permute-start.22 = (f32[192,256]{1,0:T(8,128)S(1)}, f32[192,256]{1,0:T(8,128)S(1)}, u32[]{:S(2)}, u32[]{:S(2)}) collective-permute-start(f32[192,256]{1,0:T(8,128)S(1)} %add.140), channel_id=1, source_target_pairs={{0,2},{2,0},{4,6},{6,4},{1,3},{3,1},{5,7},{7,5},{8,10},{10,8},{12,... | collective-permute-start | bytes 589832 | tf_op jit(solution)/shard_map/ppermute | solution.py:331
  185.9 6.1 %collective-permute-start.23 = (f32[192,256]{1,0:T(8,128)S(1)}, f32[192,256]{1,0:T(8,128)S(1)}, u32[]{:S(2)}, u32[]{:S(2)}) collective-permute-start(f32[192,256]{1,0:T(8,128)S(1)} %add.141), channel_id=1, source_target_pairs={{0,6},{2,4},{4,2},{6,0},{1,7},{3,5},{5,3},{7,1},{8,14},{10,12},{12... | collective-permute-start | bytes 589832 | tf_op jit(solution)/shard_map/ppermute | solution.py:332
  (12 other events, 37.6 us)

commit v3 on v2

--- a/solution.py
+++ b/solution.py
@@ -400,12 +400,13 @@
             room_for(n_dp, GLOBAL_CROPS, images, width),
             room_for(2, n_blk, 1, crop_rows),
         ],
+        60 * 1024,
     )(index, turn, own, other, got, part)
     sums = everywhere(mine, given)
     four = (4, 2, crop_rows, width)
     mine_s = scatter_chips(f_own.reshape(four), f_other.reshape(four))
     part, tot_own = call(
-        second_kernel, [VMEM, VMEM], [(VMEM, shape(1, all_teach)), (VMEM, shape(*line))]
+        second_kernel, [VMEM, VMEM], [(VMEM, shape(1, all_teach)), (VMEM, shape(*line))], (), 60 * 1024
     )(kt, sums)
     tot_other = other_core(tot_own)
     sums = everywhere(part, part)
@@ -430,11 +431,14 @@
         [SMEM, SMEM, VMEM, VMEM, VMEM, VMEM, VMEM],
         [(VMEM, shape(width, cols))],
         [room_for(2, *half), room_for(2, n_blk, 1, crop_rows)],
+        60 * 1024,
     )(index, turn, own, other, tot_own, tot_other, unit)
     next_cols, row = call(
         functools.partial(final_kernel, coef=coef),
         [SMEM, VMEM, VMEM, VMEM, VMEM, VMEM, VMEM, VMEM],
         [(VMEM, shape(n_dp, own_rows, cols)), (VMEM, shape(1, all_teach))],
+        (),
+        60 * 1024,
     )(rate[None], sums, last, weights, g, got, unit, norm)
     back = lax.all_to_all(next_cols, DP, split_axis=0, concat_axis=0, tiled=True)
     student_next = back.transpose(1, 0, 2).reshape(own_rows, own_cols)

time: 195 us -> 201 us (1.031)
  Pallas kernels: 25.3 us -> 33.4 us
  other arithmetic: 11.7 us -> 7.77 us
  waiting for transfers between devices: 65.1 us -> 67.6 us
    pallas_call x1, Pallas kernels: 6.37 us -> 8.67 us  [body(): call(student_kernel, [SMEM, SMEM, VMEM, VMEM, VMEM, VMEM], [(VMEM, messag...]
    add x2, other arithmetic: 2.31 us -> 0.11 us  [scatter_chips(): v[0] + shifted(v[1], 'x', 1) + shifted(v[2], 'x', 2) + shifted(v[3], 'x', 3)]
    pallas_call x1, Pallas kernels: 1.85 us -> 3.87 us  [body(): call(functools.partial(final_kernel, coef=coef), [SMEM, VMEM, VMEM, VMEM,...]
    unnamed x34 -> x46, local copies, waits for them, and re-layouts: 4.77 us -> 4.33 us
  transfers between devices with their start and end apart: 27 -> 27, of which waited for: 18 -> 18; matrix products, arithmetic and copies ran while one was open for 5% -> 3% of each run, Pallas kernels for 8% -> 10%
where the time goes in v3:
time: 201 us; the launch traced here: 199 us
  waiting for transfers between devices  67.6 us (34%)
  starting transfers between devices  50.2 us (25%)
  Pallas kernels  33.4 us (17%)
  blocking collectives  31.8 us (16%)
  other arithmetic  7.77 us (4%)
  local copies, waits for them, and re-layouts  6.01 us (3%)
    ppermute x13, waiting for transfers between devices, shifted(): return lax.ppermute(v, axis, [(i, (i + by) % n) for i in range(n)])  35.8 us
    all_to_all x2, blocking collectives, everywhere(): lax.all_to_all(copies, CHIPS, split_axis=0, concat_axis=0, tiled=True)  31.8 us
    ppermute x13, starting transfers between devices, shifted(): return lax.ppermute(v, axis, [(i, (i + by) % n) for i in range(n)])  17.5 us
    all_to_all x1, waiting for transfers between devices, body(): got = lax.all_to_all(pieces, DP, split_axis=0, concat_axis=0, tiled=True)  15 us
    ppermute x7, starting transfers between devices, other_core(): return lax.ppermute(v, 'c', ((0, 1), (1, 0)))  11.2 us
    pallas_call x1, Pallas kernels, body(): call(functools.partial(grad_kernel, coef=coef), [SMEM, SMEM, VMEM, VMEM,...  9.02 us
    pallas_call x1, Pallas kernels, body(): call(student_kernel, [SMEM, SMEM, VMEM, VMEM, VMEM, VMEM], [(VMEM, messag...  8.67 us
    all_to_all x1, starting transfers between devices, body(): lax.all_to_all(next_cols, DP, split_axis=0, concat_axis=0, tiled=True)  6.53 us
  transfers between devices with their start and end apart: 27, of which 18 were waited for; matrix products, arithmetic and copies ran while one was open for 3% of the time, Pallas kernels for 10%

profile of v3, /device:TPU:1, one launch (start us, length us, event | category | flops | bytes accessed | tf_op | source)
XLA Modules:
  0.0 199.0 jit_solution(4405273458751876972)
XLA Ops:
  2.0 1.9 shard_map.86
  3.8 4.6 %collective-permute-start = (f32[48,256]{1,0:T(8,128)}, f32[48,256]{1,0:T(8,128)S(1)}, u32[]{:S(2)}, u32[]{:S(2)}) collective-permute-start(f32[48,256]{1,0:T(8,128)} %shard_map.86), channel_id=1, source_target_pairs={{0,17},{1,16},{16,1},{17,0},{2,19},{3,18},{18,3},{19,2},{4,21},{5,... | collective-permute-start | bytes 147464 | tf_op jit(solution)/shard_map/ppermute | solution.py:312
  8.4 1.7 collective-permute-done
  10.9 2.8 %collective-permute-start.2 = (f32[2,48,256]{2,1,0:T(8,128)S(1)}, f32[2,48,256]{2,1,0:T(8,128)S(1)}, u32[]{:S(2)}, u32[]{:S(2)}) collective-permute-start(f32[2,48,256]{2,1,0:T(8,128)S(1)} %get-tuple-element.46), channel_id=1, source_target_pairs={{0,64},{32,96},{64,0},{96,32},{1,65},{33,97},{65,1},{97,33},{2,66}... | collective-permute-start | bytes 294920 | tf_op jit(solution)/shard_map/ppermute | solution.py:308
  16.0 1.7 collective-permute-done.1
  17.7 2.0 collective-permute-done.3
  21.1 2.6 %collective-permute-start.5 = (f32[4,2,48,256]{3,2,1,0:T(8,128)S(1)}, f32[4,2,48,256]{3,2,1,0:T(8,128)S(1)}, u32[]{:S(2)}, u32[]{:S(2)}) collective-permute-start(f32[4,2,48,256]{3,2,1,0:T(8,128)S(1)} %get-tuple-element.41), channel_id=1, source_target_pairs={{0,4},{2,6},{4,0},{6,2},{1,5},{3,7},{5,1},{7,3},{8,12},{10,14},{12... | collective-permute-start | bytes 1179656 | tf_op jit(solution)/shard_map/ppermute | solution.py:308
  24.8 4.2 %collective-permute-done.6 = f32[4,2,48,256]{3,2,1,0:T(8,128)S(1)} collective-permute-done((f32[4,2,48,256]{3,2,1,0:T(8,128)S(1)}, f32[4,2,48,256]{3,2,1,0:T(8,128)S(1)}, u32[]{:S(2)}, u32[]{:S(2)}) %collective-permute-start.6) | collective-permute-done | bytes 393248 | tf_op jit(solution)/shard_map/ppermute | solution.py:308
  29.0 9.5 %collective-permute-done.5 = f32[4,2,48,256]{3,2,1,0:T(8,128)S(1)} collective-permute-done((f32[4,2,48,256]{3,2,1,0:T(8,128)S(1)}, f32[4,2,48,256]{3,2,1,0:T(8,128)S(1)}, u32[]{:S(2)}, u32[]{:S(2)}) %collective-permute-start.5) | collective-permute-done | bytes 393248 | tf_op jit(solution)/shard_map/ppermute | solution.py:308
  41.2 2.3 %collective-permute-start.7 = (f32[4,4,2,48,256]{4,3,2,1,0:T(8,128)}, f32[4,4,2,48,256]{4,3,2,1,0:T(8,128)}, u32[]{:S(2)}, u32[]{:S(2)}) collective-permute-start(f32[4,4,2,48,256]{4,3,2,1,0:T(8,128)} %pad_maximum_fusion.1), channel_id=1, source_target_pairs={{0,8},{8,0},{1,9},{9,1},{2,10},{10,2},{3,11},{11,3},{4,12},{12,4},... | collective-permute-start | bytes 4718600 | tf_op jit(solution)/shard_map/ppermute | solution.py:292
  43.6 2.3 %shard_map.85 = f32[16,2,16,512]{3,2,1,0:T(8,128)} custom-call(f32[16,8192]{1,0:T(8,128)} %tp.1, f32[16,8192]{1,0:T(8,128)} %sp.1), custom_call_target="tpu_custom_call" | custom-call | tf_op jit(solution)/shard_map/pallas_call | solution.py:363
  45.9 3.6 %all-to-all-start = ((f32[16,2,16,512]{3,2,1,0:T(8,128)}), f32[16,2,16,512]{3,2,1,0:T(8,128)S(1)}, u32[]{:S(2)}, u32[]{:S(2)}) async-start(f32[16,2,16,512]{3,2,1,0:T(8,128)} %shard_map.85), calls=%async_computation | async-start | bytes 2097152 | tf_op jit(solution)/shard_map/all_to_all | solution.py:370
  51.4 15.0 %all-to-all-done.got.raw_in = f32[16,2,16,512]{3,2,1,0:T(8,128)S(1)} async-done(((f32[16,2,16,512]{3,2,1,0:T(8,128)}), f32[16,2,16,512]{3,2,1,0:T(8,128)S(1)}, u32[]{:S(2)}, u32[]{:S(2)}) %all-to-all-start) | async-done | bytes 1048608 | tf_op jit(solution)/shard_map/all_to_all | solution.py:370
  66.5 2.6 %shard_map.87 = (f32[512,512]{1,0:T(8,128)S(1)}, f32[1,512]{1,0:T(1,128)S(1)}) custom-call(s32[16]{0:T(128)S(1)} %fusion.18.index, s32[1]{0:T(128)} %bitcast.turn, f32[1]{0:T(128)S(6)} %add_shard_map.9.temp, f32[16,2,16,512]{3,2,1,0:T(8,128)S(1)} %all-to-all-done.got.raw_in, f32[4,8,48,256]{3,2,1,0:T(8,128)S(1)} %pad_maximum_fusion.own, ...), custom_call_target="tpu_custom_call" | custom-call | tf_op jit(solution)/shard_map/pallas_call | solution.py:377
  70.8 8.7 %shard_map.88 = (f32[1,1792]{1,0:T(1,128)}, f32[1,1792]{1,0:T(1,128)}, f32[1280,256]{1,0:T(8,128)}, f32[1280,256]{1,0:T(8,128)}, f32[256,512]{1,0:T(8,128)}, /*index=5*/f32[256,512]{1,0:T(8,128)}, f32[1,512]{1,0:T(1,128)}) custom-call(s32[16]{0:T(128)} %copy-done.6, s32[1]{0:T(128)} %bitcast.turn, f32[4,8,48,256]{3,2,1,0:T(8,128)} %copy-done, ...), custom_call_target="tpu_custom_call" | custom-call | tf_op jit(solution)/shard_map/pallas_call | solution.py:386
  80.6 2.8 %collective-permute-done.8.theirs = f32[1,1792]{1,0:T(1,128)S(1)} collective-permute-done((f32[1,1792]{1,0:T(1,128)}, f32[1,1792]{1,0:T(1,128)S(1)}, u32[]{:S(2)}, u32[]{:S(2)}) %collective-permute-start.8) | collective-permute-done | bytes 7200 | tf_op jit(solution)/shard_map/ppermute | solution.py:292
  84.1 18.9 %all_to_all.25.got = f32[64,1,1792]{2,1,0:T(1,128)} all-to-all(f32[64,1,1792]{2,1,0:T(1,128)S(1)} %shard_map.89), channel_id=1, replica_groups=mesh['x'=4,'zh'=2,'c'=2,'y'=4,'zl'=2] {'x','zh','y','zl'}, dimensions={0} | all-to-all | bytes 917504 | tf_op jit(solution)/shard_map/all_to_all | solution.py:303
  103.0 2.5 %shard_map.90 = (f32[1,512]{1,0:T(1,128)}, f32[1,1280]{1,0:T(1,128)}) custom-call(f32[512,512]{1,0:T(8,128)} %copy-done.4, f32[64,1,1792]{2,1,0:T(1,128)} %all_to_all.25.got), custom_call_target="tpu_custom_call" | custom-call | tf_op jit(solution)/shard_map/pallas_call | solution.py:408
  105.5 1.6 collective-permute-start.9
  108.9 12.9 %all_to_all.26.got = f32[64,1,512]{2,1,0:T(1,128)S(1)} all-to-all(f32[64,1,512]{2,1,0:T(1,128)S(1)} %shard_map.91), channel_id=1, replica_groups=mesh['x'=4,'zh'=2,'c'=2,'y'=4,'zl'=2] {'x','zh','y','zl'}, dimensions={0} | all-to-all | bytes 262144 | tf_op jit(solution)/shard_map/all_to_all | solution.py:303
  123.6 1.8 collective-permute-start.16
  128.5 2.5 %collective-permute-start.15 = (f32[2,160,256]{2,1,0:T(8,128)}, f32[2,160,256]{2,1,0:T(8,128)S(1)}, u32[]{:S(2)}, u32[]{:S(2)}) collective-permute-start(f32[2,160,256]{2,1,0:T(8,128)} %get-tuple-element.38), channel_id=1, source_target_pairs={{0,96},{32,0},{64,32},{96,64},{1,97},{33,1},{65,33},{97,65},{2,98}... | collective-permute-start | bytes 983048 | tf_op jit(solution)/shard_map/ppermute | solution.py:308
  134.7 2.1 %collective-permute-start.18 = (f32[2,32,256]{2,1,0:T(8,128)S(1)}, f32[2,32,256]{2,1,0:T(8,128)S(1)}, u32[]{:S(2)}, u32[]{:S(2)}) collective-permute-start(f32[2,32,256]{2,1,0:T(8,128)S(1)} %get-tuple-element.44), channel_id=1, source_target_pairs={{0,64},{32,96},{64,0},{96,32},{1,65},{33,97},{65,1},{97,33},{2,66}... | collective-permute-start | bytes 196616 | tf_op jit(solution)/shard_map/ppermute | solution.py:308
  137.4 4.6 %all-to-all-start.3 = ((f32[64,1,512]{2,1,0:T(1,128)}), f32[64,1,512]{2,1,0:T(1,128)S(1)}, u32[]{:S(2)}, u32[]{:S(2)}) async-start(f32[64,1,512]{2,1,0:T(1,128)} %shard_map.93), calls=%async_computation.3 | async-start | bytes 262144 | tf_op jit(solution)/shard_map/all_to_all | solution.py:303
  142.1 4.4 %collective-permute-done.19 = f32[2,32,256]{2,1,0:T(8,128)S(1)} collective-permute-done((f32[2,32,256]{2,1,0:T(8,128)S(1)}, f32[2,32,256]{2,1,0:T(8,128)S(1)}, u32[]{:S(2)}, u32[]{:S(2)}) %collective-permute-start.19) | collective-permute-done | bytes 65568 | tf_op jit(solution)/shard_map/ppermute | solution.py:308
  148.5 3.1 %collective-permute-start.11 = (f32[1,1280]{1,0:T(1,128)S(1)}, f32[1,1280]{1,0:T(1,128)S(1)}, u32[]{:S(2)}, u32[]{:S(2)}) collective-permute-start(f32[1,1280]{1,0:T(1,128)S(1)} %copy-done.18), channel_id=1, source_target_pairs={{0,8},{8,0},{1,9},{9,1},{2,10},{10,2},{3,11},{11,3},{4,12},{12,4},... | collective-permute-start | bytes 15368 | tf_op jit(solution)/shard_map/ppermute | solution.py:292
  152.9 9.0 %shard_map.94.g_in = f32[256,512]{1,0:T(8,128)} custom-call(s32[16]{0:T(128)} %copy-done.6, s32[1]{0:T(128)} %bitcast.turn, f32[4,8,48,256]{3,2,1,0:T(8,128)} %copy-done, f32[4,8,48,256]{3,2,1,0:T(8,128)} %bitcast.16.other, f32[1,1280]{1,0:T(1,128)} %get-tuple-element.28.tot_own, f32[1,1280]{1,0:T(1,128)} %copy-done.21, ...), custom_call_target="tpu_custom_call" | custom-call | tf_op jit(solution)/shard_map/pallas_call | solution.py:429
  162.6 3.9 %shard_map.95 = (f32[16,16,512]{2,1,0:T(8,128)}, f32[1,512]{1,0:T(1,128)}) custom-call(f32[1]{0:T(128)S(6)} %mul_shard_map.22.rate, f32[64,1,512]{2,1,0:T(1,128)} %copy-done.17, f32[512,512]{1,0:T(8,128)} %copy-done.3, f32[256,512]{1,0:T(8,128)} %get-tuple-element.27.weights, f32[256,512]{1,0:T(8,128)} %shard_map.94.g_in, f32[16,2,16,512]{3,2,1,0:T(8,128)} %copy-done.1, ...), custom_call_target="tpu_custom_call" | custom-call | tf_op jit(solution)/shard_map/pallas_call | solution.py:436
  166.5 6.5 %all-to-all-start.4 = ((f32[16,16,512]{2,1,0:T(8,128)}), f32[16,16,512]{2,1,0:T(8,128)S(1)}, u32[]{:S(2)}, u32[]{:S(2)}) async-start(f32[16,16,512]{2,1,0:T(8,128)} %get-tuple-element.31), calls=%async_computation.4 | async-start | bytes 1048576 | tf_op jit(solution)/shard_map/all_to_all | solution.py:443
  174.6 10.7 %collective-permute-done.21 = f32[192,256]{1,0:T(8,128)S(1)} collective-permute-done((f32[192,256]{1,0:T(8,128)S(1)}, f32[192,256]{1,0:T(8,128)S(1)}, u32[]{:S(2)}, u32[]{:S(2)}) %collective-permute-start.21) | collective-permute-done | bytes 196640 | tf_op jit(solution)/shard_map/ppermute | solution.py:308
  187.1 4.2 %collective-permute-done.22 = f32[192,256]{1,0:T(8,128)S(1)} collective-permute-done((f32[192,256]{1,0:T(8,128)S(1)}, f32[192,256]{1,0:T(8,128)S(1)}, u32[]{:S(2)}, u32[]{:S(2)}) %collective-permute-start.22) | collective-permute-done | bytes 196640 | tf_op jit(solution)/shard_map/ppermute | solution.py:331
  193.3 4.3 %collective-permute-done.23 = f32[192,256]{1,0:T(8,128)S(1)} collective-permute-done((f32[192,256]{1,0:T(8,128)S(1)}, f32[192,256]{1,0:T(8,128)S(1)}, u32[]{:S(2)}, u32[]{:S(2)}) %collective-permute-start.23) | collective-permute-done | bytes 196640 | tf_op jit(solution)/shard_map/ppermute | solution.py:332
  (118 shorter events, 35.8 us)
Async XLA Ops:
  3.8 6.3 %collective-permute-start = (f32[48,256]{1,0:T(8,128)}, f32[48,256]{1,0:T(8,128)S(1)}, u32[]{:S(2)}, u32[]{:S(2)}) collective-permute-start(f32[48,256]{1,0:T(8,128)} %shard_map.86), channel_id=1, source_target_pairs={{0,17},{1,16},{16,1},{17,0},{2,19},{3,18},{18,3},{19,2},{4,21},{5,... | collective-permute-start | bytes 147464 | tf_op jit(solution)/shard_map/ppermute | solution.py:312
  10.9 5.1 %collective-permute-start.2 = (f32[2,48,256]{2,1,0:T(8,128)S(1)}, f32[2,48,256]{2,1,0:T(8,128)S(1)}, u32[]{:S(2)}, u32[]{:S(2)}) collective-permute-start(f32[2,48,256]{2,1,0:T(8,128)S(1)} %get-tuple-element.46), channel_id=1, source_target_pairs={{0,64},{32,96},{64,0},{96,32},{1,65},{33,97},{65,1},{97,33},{2,66}... | collective-permute-start | bytes 294920 | tf_op jit(solution)/shard_map/ppermute | solution.py:308
  13.8 4.0 %collective-permute-start.1 = (f32[2,48,256]{2,1,0:T(8,128)S(1)}, f32[2,48,256]{2,1,0:T(8,128)S(1)}, u32[]{:S(2)}, u32[]{:S(2)}) collective-permute-start(f32[2,48,256]{2,1,0:T(8,128)S(1)} %get-tuple-element.46), channel_id=1, source_target_pairs={{0,96},{32,0},{64,32},{96,64},{1,97},{33,1},{65,33},{97,65},{2,98}... | collective-permute-start | bytes 294920 | tf_op jit(solution)/shard_map/ppermute | solution.py:308
  14.6 5.1 %collective-permute-start.3 = (f32[2,48,256]{2,1,0:T(8,128)S(1)}, f32[2,48,256]{2,1,0:T(8,128)S(1)}, u32[]{:S(2)}, u32[]{:S(2)}) collective-permute-start(f32[2,48,256]{2,1,0:T(8,128)S(1)} %get-tuple-element.46), channel_id=1, source_target_pairs={{0,32},{32,64},{64,96},{96,0},{1,33},{33,65},{65,97},{97,1},{2,34}... | collective-permute-start | bytes 294920 | tf_op jit(solution)/shard_map/ppermute | solution.py:308
  19.8 21.5 %copy-start.14 = (f32[4,2,48,256]{3,2,1,0:T(8,128)}, f32[4,2,48,256]{3,2,1,0:T(8,128)S(1)}, u32[]{:S(2)}) copy-start(f32[4,2,48,256]{3,2,1,0:T(8,128)S(1)} %get-tuple-element.41) | copy-start | bytes 1179652
  19.8 9.2 %collective-permute-start.6 = (f32[4,2,48,256]{3,2,1,0:T(8,128)S(1)}, f32[4,2,48,256]{3,2,1,0:T(8,128)S(1)}, u32[]{:S(2)}, u32[]{:S(2)}) collective-permute-start(f32[4,2,48,256]{3,2,1,0:T(8,128)S(1)} %get-tuple-element.41), channel_id=1, source_target_pairs={{0,2},{2,4},{4,6},{6,0},{1,3},{3,5},{5,7},{7,1},{8,10},{10,12},{12... | collective-permute-start | bytes 1179656 | tf_op jit(solution)/shard_map/ppermute | solution.py:308
  21.1 17.4 %collective-permute-start.5 = (f32[4,2,48,256]{3,2,1,0:T(8,128)S(1)}, f32[4,2,48,256]{3,2,1,0:T(8,128)S(1)}, u32[]{:S(2)}, u32[]{:S(2)}) collective-permute-start(f32[4,2,48,256]{3,2,1,0:T(8,128)S(1)} %get-tuple-element.41), channel_id=1, source_target_pairs={{0,4},{2,6},{4,0},{6,2},{1,5},{3,7},{5,1},{7,3},{8,12},{10,14},{12... | collective-permute-start | bytes 1179656 | tf_op jit(solution)/shard_map/ppermute | solution.py:308
  23.8 16.2 %collective-permute-start.4 = (f32[4,2,48,256]{3,2,1,0:T(8,128)S(1)}, f32[4,2,48,256]{3,2,1,0:T(8,128)S(1)}, u32[]{:S(2)}, u32[]{:S(2)}) collective-permute-start(f32[4,2,48,256]{3,2,1,0:T(8,128)S(1)} %get-tuple-element.41), channel_id=1, source_target_pairs={{0,6},{2,0},{4,2},{6,4},{1,7},{3,1},{5,3},{7,5},{8,14},{10,8},{12,... | collective-permute-start | bytes 1179656 | tf_op jit(solution)/shard_map/ppermute | solution.py:308
  41.2 25.2 %collective-permute-start.7 = (f32[4,4,2,48,256]{4,3,2,1,0:T(8,128)}, f32[4,4,2,48,256]{4,3,2,1,0:T(8,128)}, u32[]{:S(2)}, u32[]{:S(2)}) collective-permute-start(f32[4,4,2,48,256]{4,3,2,1,0:T(8,128)} %pad_maximum_fusion.1), channel_id=1, source_target_pairs={{0,8},{8,0},{1,9},{9,1},{2,10},{10,2},{3,11},{11,3},{4,12},{12,4},... | collective-permute-start | bytes 4718600 | tf_op jit(solution)/shard_map/ppermute | solution.py:292
  45.9 20.5 %all-to-all-start = ((f32[16,2,16,512]{3,2,1,0:T(8,128)}), f32[16,2,16,512]{3,2,1,0:T(8,128)S(1)}, u32[]{:S(2)}, u32[]{:S(2)}) async-start(f32[16,2,16,512]{3,2,1,0:T(8,128)} %shard_map.85), calls=%async_computation | async-start | bytes 2097152 | tf_op jit(solution)/shard_map/all_to_all | solution.py:370
  79.4 47.7 %collective-permute-start.12 = (f32[4,2,160,256]{3,2,1,0:T(8,128)}, f32[4,2,160,256]{3,2,1,0:T(8,128)S(1)}, u32[]{:S(2)}, u32[]{:S(2)}) collective-permute-start(f32[4,2,160,256]{3,2,1,0:T(8,128)} %bitcast.92), channel_id=1, source_target_pairs={{0,8},{8,0},{1,9},{9,1},{2,10},{10,2},{3,11},{11,3},{4,12},{12,4},... | collective-permute-start | bytes 3932168 | tf_op jit(solution)/shard_map/ppermute | solution.py:292
  80.5 2.9 %collective-permute-start.8 = (f32[1,1792]{1,0:T(1,128)}, f32[1,1792]{1,0:T(1,128)S(1)}, u32[]{:S(2)}, u32[]{:S(2)}) collective-permute-start(f32[1,1792]{1,0:T(1,128)} %get-tuple-element.23), channel_id=1, source_target_pairs={{0,8},{8,0},{1,9},{9,1},{2,10},{10,2},{3,11},{11,3},{4,12},{12,4},... | collective-permute-start | bytes 21512 | tf_op jit(solution)/shard_map/ppermute | solution.py:292
  84.1 37.7 %copy-start.5 = (f32[512,512]{1,0:T(8,128)S(1)}, f32[512,512]{1,0:T(8,128)}, u32[]{:S(2)}) copy-start(f32[512,512]{1,0:T(8,128)} %copy-done.4) | copy-start | bytes 3145732
  105.5 2.7 %collective-permute-start.9 = (f32[1,512]{1,0:T(1,128)}, f32[1,512]{1,0:T(1,128)S(1)}, u32[]{:S(2)}, u32[]{:S(2)}) collective-permute-start(f32[1,512]{1,0:T(1,128)} %get-tuple-element.24.mine), channel_id=1, source_target_pairs={{0,8},{8,0},{1,9},{9,1},{2,10},{10,2},{3,11},{11,3},{4,12},{12,4},... | collective-permute-start | bytes 6152 | tf_op jit(solution)/shard_map/ppermute | solution.py:292
  123.6 3.0 %collective-permute-start.16 = (f32[4,2,32,256]{3,2,1,0:T(8,128)S(1)}, f32[4,2,32,256]{3,2,1,0:T(8,128)S(1)}, u32[]{:S(2)}, u32[]{:S(2)}) collective-permute-start(f32[4,2,32,256]{3,2,1,0:T(8,128)S(1)} %bitcast.72), channel_id=1, source_target_pairs={{0,8},{8,0},{1,9},{9,1},{2,10},{10,2},{3,11},{11,3},{4,12},{12,4},... | collective-permute-start | bytes 786440 | tf_op jit(solution)/shard_map/ppermute | solution.py:292
  126.7 8.0 %collective-permute-start.17 = (f32[2,32,256]{2,1,0:T(8,128)S(1)}, f32[2,32,256]{2,1,0:T(8,128)S(1)}, u32[]{:S(2)}, u32[]{:S(2)}) collective-permute-start(f32[2,32,256]{2,1,0:T(8,128)S(1)} %get-tuple-element.42), channel_id=1, source_target_pairs={{0,32},{32,64},{64,96},{96,0},{1,33},{33,65},{65,97},{97,1},{2,34}... | collective-permute-start | bytes 196616 | tf_op jit(solution)/shard_map/ppermute | solution.py:308
  128.3 20.1 %copy-start.20 = (s32[160,2]{0,1:T(2,128)S(1)}, s32[160,2]{0,1:T(2,128)}, u32[]{:S(2)}) copy-start(s32[160,2]{0,1:T(2,128)} %param.10) | copy-start | bytes 3844
  128.3 20.1 %copy-start.18 = (f32[1,1280]{1,0:T(1,128)S(1)}, f32[1,1280]{1,0:T(1,128)}, u32[]{:S(2)}) copy-start(f32[1,1280]{1,0:T(1,128)} %get-tuple-element.28.tot_own) | copy-start | bytes 15364
  128.3 23.2 %copy-start.15 = (f32[160,256]{1,0:T(8,128)S(1)}, f32[160,256]{1,0:T(8,128)}, u32[]{:S(2)}) copy-start(f32[160,256]{1,0:T(8,128)} %sf.1) | copy-start | bytes 491524
  128.3 19.3 %collective-permute-start.13 = (f32[2,160,256]{2,1,0:T(8,128)}, f32[2,160,256]{2,1,0:T(8,128)S(1)}, u32[]{:S(2)}, u32[]{:S(2)}) collective-permute-start(f32[2,160,256]{2,1,0:T(8,128)} %get-tuple-element.37), channel_id=1, source_target_pairs={{0,32},{32,64},{64,96},{96,0},{1,33},{33,65},{65,97},{97,1},{2,34}... | collective-permute-start | bytes 983048 | tf_op jit(solution)/shard_map/ppermute | solution.py:308
  128.5 19.2 %collective-permute-start.15 = (f32[2,160,256]{2,1,0:T(8,128)}, f32[2,160,256]{2,1,0:T(8,128)S(1)}, u32[]{:S(2)}, u32[]{:S(2)}) collective-permute-start(f32[2,160,256]{2,1,0:T(8,128)} %get-tuple-element.38), channel_id=1, source_target_pairs={{0,96},{32,0},{64,32},{96,64},{1,97},{33,1},{65,33},{97,65},{2,98}... | collective-permute-start | bytes 983048 | tf_op jit(solution)/shard_map/ppermute | solution.py:308
  131.0 16.7 %collective-permute-start.14 = (f32[2,160,256]{2,1,0:T(8,128)S(1)}, f32[2,160,256]{2,1,0:T(8,128)S(1)}, u32[]{:S(2)}, u32[]{:S(2)}) collective-permute-start(f32[2,160,256]{2,1,0:T(8,128)S(1)} %get-tuple-element.39), channel_id=1, source_target_pairs={{0,64},{32,96},{64,0},{96,32},{1,65},{33,97},{65,1},{97,33},{2,66}... | collective-permute-start | bytes 983048 | tf_op jit(solution)/shard_map/ppermute | solution.py:308
  131.8 2.0 %collective-permute-start.10 = (f32[1,512]{1,0:T(1,128)S(1)}, f32[1,512]{1,0:T(1,128)S(1)}, u32[]{:S(2)}, u32[]{:S(2)}) collective-permute-start(f32[1,512]{1,0:T(1,128)S(1)} %get-tuple-element.25.mine), channel_id=1, source_target_pairs={{0,8},{8,0},{1,9},{9,1},{2,10},{10,2},{3,11},{11,3},{4,12},{12,4},... | collective-permute-start | bytes 6152 | tf_op jit(solution)/shard_map/ppermute | solution.py:292
  133.8 12.6 %collective-permute-start.19 = (f32[2,32,256]{2,1,0:T(8,128)S(1)}, f32[2,32,256]{2,1,0:T(8,128)S(1)}, u32[]{:S(2)}, u32[]{:S(2)}) collective-permute-start(f32[2,32,256]{2,1,0:T(8,128)S(1)} %get-tuple-element.43), channel_id=1, source_target_pairs={{0,96},{32,0},{64,32},{96,64},{1,97},{33,1},{65,33},{97,65},{2,98}... | collective-permute-start | bytes 196616 | tf_op jit(solution)/shard_map/ppermute | solution.py:308
  134.7 12.9 %collective-permute-start.18 = (f32[2,32,256]{2,1,0:T(8,128)S(1)}, f32[2,32,256]{2,1,0:T(8,128)S(1)}, u32[]{:S(2)}, u32[]{:S(2)}) collective-permute-start(f32[2,32,256]{2,1,0:T(8,128)S(1)} %get-tuple-element.44), channel_id=1, source_target_pairs={{0,64},{32,96},{64,0},{96,32},{1,65},{33,97},{65,1},{97,33},{2,66}... | collective-permute-start | bytes 196616 | tf_op jit(solution)/shard_map/ppermute | solution.py:308
  137.4 24.5 %all-to-all-start.3 = ((f32[64,1,512]{2,1,0:T(1,128)}), f32[64,1,512]{2,1,0:T(1,128)S(1)}, u32[]{:S(2)}, u32[]{:S(2)}) async-start(f32[64,1,512]{2,1,0:T(1,128)} %shard_map.93), calls=%async_computation.3 | async-start | bytes 262144 | tf_op jit(solution)/shard_map/all_to_all | solution.py:303
  147.8 25.3 %collective-permute-start.20 = (f32[192,256]{1,0:T(8,128)S(1)}, f32[192,256]{1,0:T(8,128)S(1)}, u32[]{:S(2)}, u32[]{:S(2)}) collective-permute-start(f32[192,256]{1,0:T(8,128)S(1)} %fusion.6), channel_id=1, source_target_pairs={{0,17},{1,16},{16,1},{17,0},{2,19},{3,18},{18,3},{19,2},{4,21},{5,... | collective-permute-start | bytes 589832 | tf_op jit(solution)/shard_map/ppermute | solution.py:312
  148.5 3.9 %collective-permute-start.11 = (f32[1,1280]{1,0:T(1,128)S(1)}, f32[1,1280]{1,0:T(1,128)S(1)}, u32[]{:S(2)}, u32[]{:S(2)}) collective-permute-start(f32[1,1280]{1,0:T(1,128)S(1)} %copy-done.18), channel_id=1, source_target_pairs={{0,8},{8,0},{1,9},{9,1},{2,10},{10,2},{3,11},{11,3},{4,12},{12,4},... | collective-permute-start | bytes 15368 | tf_op jit(solution)/shard_map/ppermute | solution.py:292
  166.5 20.5 %all-to-all-start.4 = ((f32[16,16,512]{2,1,0:T(8,128)}), f32[16,16,512]{2,1,0:T(8,128)S(1)}, u32[]{:S(2)}, u32[]{:S(2)}) async-start(f32[16,16,512]{2,1,0:T(8,128)} %get-tuple-element.31), calls=%async_computation.4 | async-start | bytes 1048576 | tf_op jit(solution)/shard_map/all_to_all | solution.py:443
  173.1 12.2 %collective-permute-start.21 = (f32[192,256]{1,0:T(8,128)S(1)}, f32[192,256]{1,0:T(8,128)S(1)}, u32[]{:S(2)}, u32[]{:S(2)}) collective-permute-start(f32[192,256]{1,0:T(8,128)S(1)} %fusion.5), channel_id=1, source_target_pairs={{0,1},{1,0},{2,3},{3,2},{4,5},{5,4},{6,7},{7,6},{8,9},{9,8},{10,11... | collective-permute-start | bytes 589832 | tf_op jit(solution)/shard_map/ppermute | solution.py:308
  185.4 5.9 %collective-permute-start.22 = (f32[192,256]{1,0:T(8,128)S(1)}, f32[192,256]{1,0:T(8,128)S(1)}, u32[]{:S(2)}, u32[]{:S(2)}) collective-permute-start(f32[192,256]{1,0:T(8,128)S(1)} %add.140), channel_id=1, source_target_pairs={{0,2},{2,0},{4,6},{6,4},{1,3},{3,1},{5,7},{7,5},{8,10},{10,8},{12,... | collective-permute-start | bytes 589832 | tf_op jit(solution)/shard_map/ppermute | solution.py:331
  191.3 6.3 %collective-permute-start.23 = (f32[192,256]{1,0:T(8,128)S(1)}, f32[192,256]{1,0:T(8,128)S(1)}, u32[]{:S(2)}, u32[]{:S(2)}) collective-permute-start(f32[192,256]{1,0:T(8,128)S(1)} %add.141), channel_id=1, source_target_pairs={{0,6},{2,4},{4,2},{6,0},{1,7},{3,5},{5,3},{7,1},{8,14},{10,12},{12... | collective-permute-start | bytes 589832 | tf_op jit(solution)/shard_map/ppermute | solution.py:332
  (18 other events, 148.6 us)
